TPU v7x, 32 devices: a whole 2x2x4 slice. The times are simulated.
32 devices in a mesh: tm: 4 (over y, x), rows: 8 (over z, core).
Axes of the slice: x: 2, y: 2, z: 4, core: 2. Of those that a mesh axis runs over, the one named last changes fastest.
Arguments:
- features: bfloat16 [48, 1280, 512], P('rows', 'tm'), may hold values from -6 to 6
- cotangent: bfloat16 [48, 1280, 512], P('rows', 'tm'), may hold values from -6 to 6
- state_bank: float32 [48, 512, 32], P('rows', 'tm'), may hold values from -6 to 6
- state_source: int32 [48], P('rows'), may hold values from 0 to 5, as said below
- master: float32 [88, 256, 256], P('tm', 'rows'), may hold values from -0.13258252 to 0.13258252
- left_stats: float32 [88, 256, 256], P('tm', 'rows'), may hold values from -7.68 to 64
- right_stats: float32 [88, 256, 256], P('tm', 'rows'), may hold values from -7.68 to 64
- left_root: float32 [88, 256, 256], P('tm', 'rows'), may hold values from -0.2 to 1.6
- right_root: float32 [88, 256, 256], P('tm'), may hold values from -0.2 to 1.6
- small_params: float32 [20, 512], replicated, may hold values from -1 to 1.5
- decay_logs: float32 [8, 32], P('tm'), may hold values from -7 to -1.5
- state_mix: float32 [2, 512, 32], P(None, 'tm'), may hold values from -0.6 to 0.6
Outputs:
- layer_out: bfloat16 [48, 1280, 512], P('rows', 'tm')
- grad_features: float32 [48, 1280, 512], P('rows', 'tm')
- grad_state: float32 [48, 512, 32], P('rows', 'tm')
- grad_blocks: float32 [88, 256, 256], P('tm', 'rows')
- new_left: float32 [88, 256, 256], P('tm', 'rows')
- new_right: float32 [88, 256, 256], P('tm', 'rows')
- new_master: float32 [88, 256, 256], P('tm', 'rows')
- new_copy: bfloat16 [88, 256, 256], P('tm', 'rows')
- grad_small: float32 [20, 512], P(None, 'tm')
- new_small: float32 [20, 512], P(None, 'tm')
- grad_decay: float32 [8, 32], P('tm')
- grad_mix: float32 [2, 512, 32], P(None, 'tm')
- new_decay: float32 [8, 32], P('tm')
- new_mix: float32 [2, 512, 32], P(None, 'tm')
Inputs may be any that keep to these rules, and one draw needn't show every extreme that they name: `state_source`: within each aligned block of 6 rows the values are a permutation of 0 to 5.
All inputs are finite; a program needn't handle non-finite values.
Results may differ from a plain program's by a relative error of at most 0.018.
Values may be sent and summed in bfloat16 or wider, within the bound.
A program may use at most 320 MiB of HBM per device.

v0:
```python
from functools import partial
import math

import jax
import jax.numpy as jnp
from jax import lax
from jax.sharding import PartitionSpec as P

D = 512
FF = 2048
NST = 32
KW = 15
BS = 256


precise = lax.Precision.HIGHEST
three_pass = lax.Precision.HIGH
rate_blocks = 0.1
rate_small = 0.5


def with_halo(block, sides, width):
    for axis, dim in sides:
        count = lax.axis_size(axis)
        forward = [(i, i + 1) for i in range(count - 1)]
        backward = [(target, source) for source, target in forward]
        low = lax.ppermute(
            lax.slice_in_dim(block, block.shape[dim] - width, None, axis=dim), axis, forward
        )
        high = lax.ppermute(lax.slice_in_dim(block, 0, width, axis=dim), axis, backward)
        block = jnp.concatenate([low, block, high], axis=dim)
    return block


def layer_norm(values, scales):
    center = values - jnp.mean(values, axis=-1, keepdims=True)
    spread = jnp.mean(center * center, axis=-1, keepdims=True)
    return center * lax.rsqrt(spread + 1e-05) * scales


def norm_back(values, scales, incoming):
    unused, pull_back = jax.vjp(layer_norm, values, scales)
    return pull_back(incoming)


def gating(values):
    half_width = values.shape[-1] // 2
    return values[..., :half_width] * jax.nn.sigmoid(values[..., half_width:])


def silu_back(values, incoming):
    return jax.vjp(jax.nn.silu, values)[1](incoming)[0]


def gating_back(values, incoming):
    return jax.vjp(gating, values)[1](incoming)[0]


def matmul(first, second):
    return jnp.dot(first, second, preferred_element_type=jnp.float32)


def inner_rows(first, second):
    return lax.dot_general(
        first, second, (((0,), (0,)), ((), ())), preferred_element_type=jnp.float32
    )


def inner_cols(first, second):
    return lax.dot_general(
        first, second, (((1,), (1,)), ((), ())), preferred_element_type=jnp.float32
    )


def to_matrix(block_stack, first, rows_count, cols_count):
    blocks_down = rows_count // BS
    blocks_across = cols_count // BS
    picked = block_stack[first : first + blocks_down * blocks_across]
    picked = picked.reshape(blocks_down, blocks_across, BS, BS).transpose(0, 2, 1, 3)
    return picked.reshape(rows_count, cols_count)


def to_blocks(matrix):
    rows_count, cols_count = matrix.shape
    return (
        matrix.reshape(rows_count // BS, BS, cols_count // BS, BS)
        .transpose(0, 2, 1, 3)
        .reshape(-1, BS, BS)
    )


def matrices(block_stack):
    ffn_count = D // BS * (FF // BS)
    mix_count = (D // BS) ** 2
    base_index = 4 * ffn_count
    return (
        to_matrix(block_stack, 0, D, FF),
        to_matrix(block_stack, ffn_count, FF, D),
        to_matrix(block_stack, 2 * ffn_count, D, FF),
        to_matrix(block_stack, 3 * ffn_count, FF, D),
        to_matrix(block_stack, base_index, D, D),
        to_matrix(block_stack, base_index + mix_count, D, 2 * D),
        to_matrix(block_stack, base_index + 3 * mix_count, D, 2 * D),
        to_matrix(block_stack, base_index + 5 * mix_count, D, D),
    )


def dft_tables(frames):
    period = 2 * frames - 1
    counter = jnp.arange(frames, dtype=jnp.int32)
    phase = (counter[:, None] * counter[None, :] % period).astype(jnp.float32) * (
        2.0 * math.pi / period
    )
    cosine = jnp.cos(phase)
    sine = jnp.sin(phase)
    forward_table = jnp.concatenate([cosine, -sine], axis=1)
    table_high = forward_table.astype(jnp.bfloat16)
    table_rest = (forward_table - table_high.astype(jnp.float32)).astype(jnp.bfloat16)
    split_table = jnp.concatenate([table_high, table_rest], axis=1)
    weighting = jnp.where(counter == 0, 1.0, 2.0).astype(jnp.float32) / period
    inverse_table = jnp.concatenate(
        [cosine * weighting[:, None], -sine * weighting[:, None]], axis=0
    )
    return (forward_table, split_table, inverse_table)


def conv_local(
    inputs_here,
    bank_rows,
    log_rates,
    mix_terms,
    selector,
    forward_table,
    split_table,
    inverse_table,
):
    row_count, frames, width = inputs_here.shape
    head_count = log_rates.shape[0]
    decay_rates = jnp.exp(log_rates)
    positions = jnp.arange(frames, dtype=jnp.float32)
    decay_now = jnp.exp(-decay_rates[:, :, None] * positions)
    decay_next = jnp.exp(-decay_rates[:, :, None] * (positions + 1.0))
    coupling = (mix_terms[0] * mix_terms[1]).reshape(head_count, width // head_count, NST)
    kernel = jnp.einsum("hdn,hnt->hdt", coupling, decay_now, precision=precise).reshape(
        width, frames
    )
    kernel_hat = jnp.dot(kernel, forward_table, precision=precise)
    both_hat = jnp.einsum(
        "rtc,tk->rck",
        inputs_here.astype(jnp.bfloat16),
        split_table,
        preferred_element_type=jnp.float32,
    )
    input_hat = both_hat[..., : 2 * frames] + both_hat[..., 2 * frames :]
    real_in = input_hat[..., :frames]
    imag_in = input_hat[..., frames:]
    real_kernel = kernel_hat[:, :frames]
    imag_kernel = kernel_hat[:, frames:]
    output_hat = jnp.concatenate(
        [
            real_in * real_kernel - imag_in * imag_kernel,
            real_in * imag_kernel + imag_in * real_kernel,
        ],
        axis=-1,
    )
    mixed = jnp.einsum("rck,kt->rtc", output_hat, inverse_table, precision=three_pass)
    starts = jnp.einsum("rs,scn->rcn", selector, bank_rows, precision=precise)
    carried = (mix_terms[1][None] * starts).reshape(row_count, head_count, width // head_count, NST)
    carried_out = jnp.einsum("rhdn,hnt->rthd", carried, decay_next, precision=precise)
    return mixed + carried_out.reshape(row_count, frames, width)


def ffn_forward(values, scales, weight_in, weight_out):
    normed = layer_norm(values, scales).astype(jnp.bfloat16)
    inner = matmul(normed, weight_in)
    activated = jax.nn.silu(inner).astype(jnp.bfloat16)
    return (0.5 * matmul(activated, weight_out), (normed, inner, activated))


def ffn_backward(values, scales, weight_in, weight_out, saved, incoming):
    normed, inner, activated = saved
    grad_outer = (0.5 * incoming).astype(jnp.bfloat16)
    grad_weight_out = inner_rows(activated, grad_outer)
    grad_act = inner_cols(grad_outer, weight_out)
    grad_inner = silu_back(inner, grad_act).astype(jnp.bfloat16)
    grad_weight_in = inner_rows(normed, grad_inner)
    grad_normed = inner_cols(grad_inner, weight_in)
    grad_values, grad_scales = norm_back(values, scales, grad_normed)
    return (incoming + grad_values, grad_scales, grad_weight_in, grad_weight_out)


def body(
    features,
    cotangent,
    state_bank,
    state_source,
    master,
    left_stats,
    right_stats,
    left_root,
    right_root,
    small_params,
    decay_logs,
    state_mix,
):
    row_count, frame_count, width = features.shape
    token_count = row_count * frame_count
    margin = (KW - 1) // 2
    scaling = 1.0 / math.sqrt(token_count * lax.axis_size("tm") * lax.axis_size("rows"))
    copy_part = master.astype(jnp.bfloat16)
    partial_stack = lax.all_gather(copy_part, "rows", axis=1, tiled=True)
    block_stack = lax.all_gather(partial_stack, "tm", axis=0, tiled=True)
    ffa_in, ffa_out, ffb_in, ffb_out, mixer_in, mixer_out, conv_in, conv_out = matrices(block_stack)
    kernel_rows = small_params[5:]
    stream_zero = features.astype(jnp.float32).reshape(token_count, width)
    branch_one, saved_one = ffn_forward(stream_zero, small_params[0], ffa_in, ffa_out)
    stream_one = stream_zero + branch_one
    normed_mixer = layer_norm(stream_one, small_params[1]).astype(jnp.bfloat16)
    mixer_input = (
        matmul(normed_mixer, mixer_in).astype(jnp.bfloat16).reshape(row_count, frame_count, width)
    )
    channel_in = lax.all_to_all(mixer_input, "tm", split_axis=2, concat_axis=1, tiled=True)
    forward_table, split_table, inverse_table = dft_tables(channel_in.shape[1])
    selector = (state_source[:, None] == jnp.arange(row_count, dtype=jnp.int32)[None, :]).astype(
        jnp.float32
    )
    mixer_local = partial(
        conv_local,
        selector=selector,
        forward_table=forward_table,
        split_table=split_table,
        inverse_table=inverse_table,
    )
    channel_out, mixer_pull = jax.vjp(
        mixer_local, channel_in.astype(jnp.float32), state_bank, decay_logs, state_mix
    )
    mixer_result = lax.all_to_all(
        channel_out.astype(jnp.bfloat16), "tm", split_axis=1, concat_axis=2, tiled=True
    ).reshape(token_count, width)
    gated = matmul(mixer_result, mixer_out)
    stream_two = stream_one + gating(gated)
    normed_conv = layer_norm(stream_two, small_params[2]).astype(jnp.bfloat16)
    pointwise = matmul(normed_conv, conv_in)
    gated_units = gating(pointwise).astype(jnp.bfloat16).reshape(row_count, frame_count, width)
    padded = with_halo(gated_units, (("tm", 1),), margin)
    padded_full = padded.astype(jnp.float32)
    depthwise = kernel_rows[0] * padded_full[:, 0:frame_count]
    for offset in range(1, KW):
        depthwise = depthwise + kernel_rows[offset] * padded_full[:, offset : offset + frame_count]
    depth_flat = depthwise.reshape(token_count, width)
    activated_conv = jax.nn.silu(depth_flat).astype(jnp.bfloat16)
    stream_three = stream_two + matmul(activated_conv, conv_out)
    branch_four, saved_four = ffn_forward(stream_three, small_params[3], ffb_in, ffb_out)
    stream_four = stream_three + branch_four
    layer_out, out_pull = jax.vjp(layer_norm, stream_four, small_params[4])
    grad_four, grad_gain_out = out_pull(cotangent.astype(jnp.float32).reshape(token_count, width))
    grad_three, grad_gain_b, grad_fb_in, grad_fb_out = ffn_backward(
        stream_three, small_params[3], ffb_in, ffb_out, saved_four, grad_four
    )
    grad_conv_out = grad_three.astype(jnp.bfloat16)
    grad_weight_conv_out = inner_rows(activated_conv, grad_conv_out)
    grad_activated = inner_cols(grad_conv_out, conv_out)
    grad_depth = (
        silu_back(depth_flat, grad_activated)
        .astype(jnp.bfloat16)
        .reshape(row_count, frame_count, width)
    )
    grad_padded = with_halo(grad_depth, (("tm", 1),), margin).astype(jnp.float32)
    grad_depth_full = grad_depth.astype(jnp.float32)
    grad_units = kernel_rows[0] * grad_padded[:, 2 * margin : 2 * margin + frame_count]
    kernel_grads = [jnp.sum(grad_depth_full * padded_full[:, 0:frame_count], axis=(0, 1))]
    for offset in range(1, KW):
        grad_units = (
            grad_units
            + kernel_rows[offset]
            * grad_padded[:, 2 * margin - offset : 2 * margin - offset + frame_count]
        )
        kernel_grads.append(
            jnp.sum(grad_depth_full * padded_full[:, offset : offset + frame_count], axis=(0, 1))
        )
    grad_pointwise = gating_back(pointwise, grad_units.reshape(token_count, width)).astype(
        jnp.bfloat16
    )
    grad_weight_conv_in = inner_rows(normed_conv, grad_pointwise)
    grad_values, grad_gain_c = norm_back(
        stream_two, small_params[2], inner_cols(grad_pointwise, conv_in)
    )
    grad_two = grad_three + grad_values
    grad_gated = gating_back(gated, grad_two).astype(jnp.bfloat16)
    grad_weight_mixer_out = inner_rows(mixer_result, grad_gated)
    grad_mixer_frames = (
        inner_cols(grad_gated, mixer_out)
        .astype(jnp.bfloat16)
        .reshape(row_count, frame_count, width)
    )
    grad_channel_out = lax.all_to_all(
        grad_mixer_frames, "tm", split_axis=2, concat_axis=1, tiled=True
    )
    grad_channel_in, grad_state, grad_logs, grad_mix_terms = mixer_pull(
        grad_channel_out.astype(jnp.float32)
    )
    grad_input_frames = lax.all_to_all(
        grad_channel_in.astype(jnp.bfloat16), "tm", split_axis=1, concat_axis=2, tiled=True
    ).reshape(token_count, width)
    grad_weight_mixer_in = inner_rows(normed_mixer, grad_input_frames)
    grad_values, grad_gain_s = norm_back(
        stream_one, small_params[1], inner_cols(grad_input_frames, mixer_in)
    )
    grad_one = grad_two + grad_values
    grad_zero, grad_gain_a, grad_fa_in, grad_fa_out = ffn_backward(
        stream_zero, small_params[0], ffa_in, ffa_out, saved_one, grad_one
    )
    grad_stack = (
        jnp.concatenate(
            [
                to_blocks(grad_fa_in),
                to_blocks(grad_fa_out),
                to_blocks(grad_fb_in),
                to_blocks(grad_fb_out),
                to_blocks(grad_weight_mixer_in),
                to_blocks(grad_weight_mixer_out),
                to_blocks(grad_weight_conv_in),
                to_blocks(grad_weight_conv_out),
            ],
            axis=0,
        )
        * scaling
    )
    small_grads = (
        jnp.concatenate(
            [
                jnp.stack([grad_gain_a, grad_gain_s, grad_gain_c, grad_gain_b, grad_gain_out]),
                jnp.stack(kernel_grads),
            ],
            axis=0,
        )
        * scaling
    )
    rows_part = lax.psum_scatter(
        grad_stack.astype(jnp.bfloat16), "rows", scatter_dimension=1, tiled=True
    )
    owned, small_part = (
        lax.psum_scatter(rows_part, "tm", scatter_dimension=0, tiled=True).astype(jnp.float32),
        lax.psum_scatter(
            small_grads.astype(jnp.bfloat16), "tm", scatter_dimension=1, tiled=True
        ).astype(jnp.float32),
    )
    decay_sum, mix_sum, small_sum = lax.psum(
        (grad_logs * scaling, grad_mix_terms * scaling, small_part), "rows"
    )
    full_grad = lax.all_gather(owned.astype(jnp.bfloat16), "rows", axis=1, tiled=True).astype(
        owned.dtype
    )
    slice_rows = owned.shape[1]
    grad_columns = lax.dynamic_slice_in_dim(
        full_grad, lax.axis_index("rows") * slice_rows, slice_rows, 2
    )
    new_left = 0.5 * left_stats + 0.5 * jnp.einsum(
        "bik,bjk->bij", owned, full_grad, precision=precise
    )
    new_right = 0.5 * right_stats + 0.5 * jnp.einsum(
        "bki,bkj->bij", grad_columns, full_grad, precision=precise
    )
    left_side = jnp.einsum("bij,bjk->bik", left_root, full_grad, precision=precise)
    step_value = jnp.einsum("bik,bkl->bil", left_side, right_root, precision=precise)
    new_master = master - rate_blocks * step_value
    small_width = small_sum.shape[1]
    own_small = lax.dynamic_slice_in_dim(
        small_params, lax.axis_index("tm") * small_width, small_width, 1
    )
    new_small = own_small - rate_small * small_sum
    new_decay = decay_logs - rate_small * decay_sum
    new_mix = state_mix - rate_small * mix_sum
    return (
        layer_out.astype(jnp.bfloat16).reshape(row_count, frame_count, width),
        grad_zero.reshape(row_count, frame_count, width),
        grad_state,
        owned,
        new_left,
        new_right,
        new_master,
        new_master.astype(jnp.bfloat16),
        small_sum,
        new_small,
        decay_sum,
        mix_sum,
        new_decay,
        new_mix,
    )


def solution(mesh):
    return jax.shard_map(
        body,
        mesh=mesh,
        in_specs=(
            P("rows", "tm", None),
            P("rows", "tm", None),
            P("rows", "tm", None),
            P("rows"),
            P("tm", "rows", None),
            P("tm", "rows", None),
            P("tm", "rows", None),
            P("tm", "rows", None),
            P("tm", None, None),
            P(),
            P("tm", None),
            P(None, "tm", None),
        ),
        out_specs=(
            P("rows", "tm", None),
            P("rows", "tm", None),
            P("rows", "tm", None),
            P("tm", "rows", None),
            P("tm", "rows", None),
            P("tm", "rows", None),
            P("tm", "rows", None),
            P("tm", "rows", None),
            P(None, "tm"),
            P(None, "tm"),
            P("tm", None),
            P(None, "tm", None),
            P("tm", None),
            P(None, "tm", None),
        ),
        check_vma=False,
    )
```

profile of v0, /device:TPU:0, one launch (start us, length us, event | category | flops | bytes accessed | tf_op | source)
XLA Modules:
  0.0 1053.2 jit_solution(16982755594584130233)
XLA Ops:
  9.4 39.7 %all-gather.4.cloned.1.call-done = bf16[22,256,256]{2,1,0:T(8,128)(2,1)} async-done(((bf16[22,32,256]{2,1,0:T(8,128)(2,1)}), bf16[22,256,256]{2,1,0:T(8,128)(2,1)}) %all-gather.4.cloned.1.call-update) | async-done | bytes 2883600 | tf_op jit(solution)/shard_map/all_gather | solution.py:211
  70.0 26.9 %sine_negate_fusion = (f32[1280,1280]{1,0:T(8,128)S(1)}, f32[1280,1280]{1,0:T(8,128)S(1)}) fusion(), kind=kLoop, calls=%fused_computation.60 | loop fusion | flops 16384000 | bytes 13107200 | tf_op jit(solution)/shard_map/neg | solution.py:122
  97.0 7.0 fusion.31
  111.4 52.3 %all-gather.6.cloned.1.call-done = bf16[88,256,256]{2,1,0:T(8,128)(2,1)} async-done(((bf16[22,256,256]{2,1,0:T(8,128)(2,1)}), bf16[88,256,256]{2,1,0:T(8,128)(2,1)}) %all-gather.6.cloned.1.call-update) | async-done | bytes 11534352 | tf_op jit(solution)/shard_map/all_gather | solution.py:212
  180.0 9.7 multiply_convert_fusion.2
  205.7 28.6 %broadcast_multiply_fusion.1 = (f32[1280,1280]{1,0:T(8,128)}, f32[1280,1280]{1,0:T(8,128)}) fusion(f32[1280]{0:T(1024)S(1)} %select_multiply_fusion), kind=kLoop, calls=%fused_computation.184 | loop fusion | flops 19660800 | bytes 13112320 | tf_op jit(solution)/shard_map/mul | solution.py:122
  234.2 7.9 all-to-all-done
  246.9 16.8 %fusion.18 = f32[6,128,5120]{2,1,0:T(8,128)} fusion(bf16[6,1280,128]{2,1,0:T(8,128)(2,1)S(1)} %bitcast.422, bf16[1280,2560]{1,0:T(8,128)(2,1)} %subtract_convert_fusion, bf16[1280,2560]{1,0:T(8,128)(2,1)} %fusion.32), kind=kOutput, calls=%fused_computation.49 | convolution fusion | flops 10092544000 | bytes 30801920 | tf_op jit(solution)/shard_map/jvp(rtc,tk->rck)/dot_general | solution.py:148
  263.7 7.1 slice_add_fusion
  276.5 35.6 %fusion.73 = bf16[6,1280,128]{2,1,0:T(8,128)(2,1)S(1)} fusion(f32[6,1280,128]{2,1,0:T(8,128)S(1)} %copy-done.52, f32[6,128,1280]{2,1,0:T(8,128)} %get-tuple-element.127, f32[6,128,1280]{2,1,0:T(8,128)S(1)} %get-tuple-element.126, f32[1280,1280]{1,0:T(8,128)} %get-tuple-element.169, f32[1280,1280]{1,0:T(8,128)} %get-tuple-element.168), kind=kOutput, calls=%fused_computation.136 | convolution fusion | flops 15106703360 | bytes 26869760 | tf_op jit(solution)/shard_map/jvp(rck,kt->rtc)/dot_general | solution.py:166
  312.1 8.5 copy.192
  330.4 24.2 %all-to-all-done.1 = bf16[6,1280,128]{2,0,1:T(8,128)(2,1)S(1)} async-done(((bf16[6,1280,128]{2,0,1:T(8,128)(2,1)}), bf16[6,1280,128]{2,0,1:T(8,128)(2,1)S(1)}, u32[]{:S(2)}, u32[]{:S(2)}) %all-to-all-start.1) | async-done | bytes 1966112 | tf_op jit(solution)/shard_map/all_to_all | solution.py:237
  407.2 8.8 multiply_convert_fusion.9
  428.0 10.1 multiply_convert_fusion.1
  449.3 14.8 %fusion.2 = bf16[1920,2048]{1,0:T(8,128)(2,1)} fusion(f32[1920,2048]{1,0:T(8,128)} %get-tuple-element.179, bf16[2048,512]{0,1:T(8,128)(2,1)S(1)} %bitcast.412, f32[1920,512]{0,1:T(8,128)S(1)} %get-tuple-element.109, f32[1920]{0:T(1024)S(1)} %negate_multiply_fusion.4), kind=kOutput, calls=%fused_computation.21 | convolution fusion | flops 4068802560 | bytes 29629952 | tf_op jit(solution)/shard_map/dot_general | solution.py:70
  464.1 8.6 multiply_reduce_fusion.5
  490.3 8.1 fusion.167
  503.0 8.0 fusion.53
  530.2 6.7 fusion.37
  560.7 9.6 fusion.120
  570.3 20.0 %all-to-all-done.2 = bf16[6,320,512]{1,0,2:T(8,128)(2,1)} async-done(((bf16[6,320,512]{1,0,2:T(8,128)(2,1)}), bf16[6,320,512]{1,0,2:T(8,128)(2,1)}, u32[]{:S(2)}, u32[]{:S(2)}) %all-to-all-start.2) | async-done | bytes 1966112 | tf_op jit(solution)/shard_map/all_to_all | solution.py:296
  599.4 14.3 %fusion.16 = f32[6,128,2560]{2,1,0:T(8,128)S(1)} fusion(f32[1280,1280]{1,0:T(8,128)} %get-tuple-element.169, f32[1280,1280]{1,0:T(8,128)} %get-tuple-element.168, bf16[6,1280,128]{1,2,0:T(8,128)(2,1)} %copy.214), kind=kOutput, calls=%fused_computation.46 | convolution fusion | flops 15102771200 | bytes 22937600 | tf_op jit(solution)/shard_map/transpose(jvp(rck,kt->rtc))/dot_general | solution.py:166
  623.9 21.3 %fusion.79 = bf16[6,1280,128]{1,2,0:T(8,128)(2,1)S(1)} fusion(bf16[1280,2560]{1,0:T(8,128)(2,1)} %subtract_convert_fusion, bf16[1280,2560]{1,0:T(8,128)(2,1)} %fusion.32, f32[6,128,2560]{2,1,0:T(8,128)} %pad_add_fusion), kind=kOutput, calls=%fused_computation.185 | convolution fusion | flops 10097459200 | bytes 22937600 | tf_op jit(solution)/shard_map/transpose(jvp(rtc,tk->rck))/dot_general | solution.py:148
  703.5 9.7 fusion.187
  723.9 17.8 %fusion.8 = (bf16[2048,1920]{0,1:T(8,128)(2,1)}, f32[1920,2048]{1,0:T(8,128)}) fusion(f32[1920,2048]{1,0:T(8,128)} %get-tuple-element.171, bf16[1920,512]{0,1:T(8,128)(2,1)S(1)} %multiply_convert_fusion.5, bf16[2048,512]{0,1:T(8,128)(2,1)S(1)} %bitcast.407), kind=kOutput, calls=%fused_computation.27 | convolution fusion | flops 4065853440 | bytes 43384832 | tf_op jit(solution)/shard_map/dot_general | solution.py:70
  741.8 10.7 %copy.263 = bf16[2048,1920]{1,0:T(8,128)(2,1)} copy(bf16[2048,1920]{0,1:T(8,128)(2,1)} %get-tuple-element.188) | data formatting | bytes 15728640 | tf_op jit(solution)/shard_map/dot_general | solution.py:64
  752.5 17.1 %multiply_reduce_fusion.9 = (f32[1920]{0:T(1024)S(1)}, f32[1920,512]{0,1:T(8,128)S(1)}) fusion(f32[1920,512]{0,1:T(8,128)} %copy.178, f32[1920]{0:T(1024)S(1)} %copy-done.98, f32[512]{0:T(512)S(1)} %bitcast.439, bf16[512,2048]{1,0:T(8,128)(2,1)S(1)} %bitcast.405, f32[1920,2048]{1,0:T(8,128)} %get-tuple-element.171, f32[1920,2048]{1,0:T(8,128)} %get-tuple-element.189), kind=kOutput, calls=%fused_computation.149 | convolution fusion | flops 4069783552 | bytes 41436160 | tf_op jit(solution)/shard_map/dot_general | solution.py:70
  798.0 120.9 %reduce-scatter.6.cloned.1.call-done = bf16[88,32,256]{2,1,0:T(8,128)(2,1)} async-done(((bf16[88,256,256]{2,1,0:T(8,128)(2,1)}), bf16[88,32,256]{2,1,0:T(8,128)(2,1)}) %reduce-scatter.6.cloned.1.call-update) | async-done | bytes 1441808 | tf_op jit(solution)/shard_map/reduce_scatter | solution.py:339
  919.1 27.1 %fusion.52 = (f32[512]{0:T(512)S(1)}, f32[512]{0:T(512)S(1)}, f32[512]{0:T(512)S(1)}, f32[512]{0:T(512)S(1)}, f32[512]{0:T(512)S(1)}, /*index=5*/f32[512]{0:T(51...) fusion(bf16[6,320,512]{2,1,0:T(8,128)(2,1)S(1)} %bitcast.352, ...), kind=kLoop, calls=%fused_computation.97 | loop fusion | flops 30466560 | bytes 60979200 | tf_op jit(solution)/shard_map/reduce_sum | solution.py:279
  968.7 16.2 %fusion.30 = f32[128,1280]{1,0:T(8,128)S(1)} fusion(f32[1280,1280]{1,0:T(8,128)} %copy-done.2, f32[1280,1280]{1,0:T(8,128)} %copy-done.3, f32[128,1280]{1,0:T(8,128)S(1)} %add_any.121, f32[128,1280]{1,0:T(8,128)S(1)} %add_any.120), kind=kOutput, calls=%fused_computation.66 | convolution fusion | flops 5036769280 | bytes 15073280 | tf_op jit(solution)/shard_map/transpose(jvp())/dot_general | solution.py:147
  998.7 29.4 %all-reduce.13 = (f32[20,128]{1,0:T(8,128)S(1)}, f32[2,32]{1,0:T(2,128)S(1)}, f32[2,128,32]{1,2,0:T(8,128)S(1)}) all-reduce(bf16[20,128]{1,0:T(8,128)(2,1)S(1)} %copy.265, f32[2,32]{1,0:T(2,128)S(1)} %multiply_multiply_fusion.5, f32[2,128,32]{1,2,0:T(8,128)S(1)} %add_multiply_fusion), channel_id=1, replica_groups=mesh['tm'=4,'rows'=8] {'rows'}, use_global_device_ids=true, to_apply=%region_43.44 | all-reduce | flops 10816 | bytes 81408 | tf_op jit(solution)/shard_map/psum | solution.py:348
  1035.0 7.2 fusion.185
  (509 shorter events, 386.1 us)
Async XLA Ops:
  7.2 1024.4 %copy-start = (f32[22,32,256]{2,1,0:T(8,128)S(1)}, f32[22,32,256]{2,1,0:T(8,128)}, u32[]{:S(2)}) copy-start(f32[22,32,256]{2,1,0:T(8,128)} %param.19) | copy-start | bytes 2162692
  7.2 42.0 %copy-start.106 = (f32[20,512]{1,0:T(8,128)S(1)}, f32[20,512]{1,0:T(8,128)}, u32[]{:S(2)}) copy-start(f32[20,512]{1,0:T(8,128)} %param.21) | copy-start | bytes 122884
  7.2 42.0 %copy-start.84 = (f32[2,128,32]{1,2,0:T(8,128)S(1)}, f32[2,128,32]{1,2,0:T(8,128)}, u32[]{:S(2)}) copy-start(f32[2,128,32]{1,2,0:T(8,128)} %param.23) | copy-start | bytes 98308
  7.2 42.1 %copy-start.142 = (s32[6]{0:T(128)S(1)}, s32[6]{0:T(128)}, u32[]{:S(2)}) copy-start(s32[6]{0:T(128)} %param.15) | copy-start | bytes 76
  7.2 42.1 %copy-start.88 = (f32[6,128,32]{1,2,0:T(8,128)S(1)}, f32[6,128,32]{1,2,0:T(8,128)}, u32[]{:S(2)}) copy-start(f32[6,128,32]{1,2,0:T(8,128)} %param.14) | copy-start | bytes 294916
  7.2 43.2 %copy-start.26 = (bf16[6,320,512]{2,1,0:T(8,128)(2,1)S(1)}, bf16[6,320,512]{2,1,0:T(8,128)(2,1)}, u32[]{:S(2)}) copy-start(bf16[6,320,512]{2,1,0:T(8,128)(2,1)} %param.12) | copy-start | bytes 5898244
  7.3 41.9 %all-gather.4.cloned.1.call-start = ((), (), s32[]{:S(2)}) async-start(), calls=%async_computation.7 | async-start | bytes 3244032 | tf_op jit(solution)/shard_map/all_gather | solution.py:211
  9.4 154.3 %all-gather.6.cloned.1.call-start = ((), (), s32[]{:S(2)}) async-start(), calls=%async_computation.8 | async-start | bytes 14417920 | tf_op jit(solution)/shard_map/all_gather | solution.py:212
  67.5 127.3 %copy-start.116 = (f32[1,512]{1,0:T(1,128)}, f32[1,512]{1,0:T(1,128)S(1)}, u32[]{:S(2)}) copy-start(f32[1,512]{1,0:T(1,128)S(1)} %get-tuple-element.161) | copy-start | bytes 6148
  67.5 295.0 %copy-start.118 = (f32[1,512]{1,0:T(1,128)}, f32[1,512]{1,0:T(1,128)S(1)}, u32[]{:S(2)}) copy-start(f32[1,512]{1,0:T(1,128)S(1)} %get-tuple-element.159) | copy-start | bytes 6148
  104.9 165.9 %copy-start.45 = (f32[128,1280]{1,0:T(8,128)}, f32[128,1280]{1,0:T(8,128)S(1)}, u32[]{:S(2)}) copy-start(f32[128,1280]{1,0:T(8,128)S(1)} %get-tuple-element.139) | copy-start | bytes 1966084
  200.8 41.2 %all-to-all-start = ((bf16[6,320,512]{1,0,2:T(8,128)(2,1)}), bf16[6,320,512]{1,0,2:T(8,128)(2,1)}, u32[]{:S(2)}, u32[]{:S(2)}) async-start(bf16[6,320,512]{1,0,2:T(8,128)(2,1)} %copy.180), calls=%async_computation | async-start | bytes 6291456 | tf_op jit(solution)/shard_map/all_to_all | solution.py:222
  320.6 34.0 %all-to-all-start.1 = ((bf16[6,1280,128]{2,0,1:T(8,128)(2,1)}), bf16[6,1280,128]{2,0,1:T(8,128)(2,1)S(1)}, u32[]{:S(2)}, u32[]{:S(2)}) async-start(bf16[6,1280,128]{2,0,1:T(8,128)(2,1)} %copy.192), calls=%async_computation.1 | async-start | bytes 5242880 | tf_op jit(solution)/shard_map/all_to_all | solution.py:237
  375.5 30.9 %collective-permute-start = (bf16[6,7,512]{2,1,0:T(8,128)(2,1)}, bf16[6,7,512]{2,1,0:T(8,128)(2,1)S(1)}, u32[]{:S(2)}, u32[]{:S(2)}) collective-permute-start(bf16[6,7,512]{2,1,0:T(8,128)(2,1)} %get-tuple-element.137), channel_id=1, source_target_pairs={{0,8},{8,16},{16,24},{1,9},{9,17},{17,25},{2,10},{10,18},{18,26},{... | collective-permute-start | bytes 129032 | tf_op jit(solution)/shard_map/ppermute | solution.py:27
  378.9 27.6 %collective-permute-start.1 = (bf16[6,7,512]{2,1,0:T(8,128)(2,1)S(1)}, bf16[6,7,512]{2,1,0:T(8,128)(2,1)S(1)}, u32[]{:S(2)}, u32[]{:S(2)}) collective-permute-start(bf16[6,7,512]{2,1,0:T(8,128)(2,1)S(1)} %get-tuple-element.138), channel_id=1, source_target_pairs={{8,0},{16,8},{24,16},{9,1},{17,9},{25,17},{10,2},{18,10},{26,18},{... | collective-permute-start | bytes 129032 | tf_op jit(solution)/shard_map/ppermute | solution.py:30
  425.0 47.8 %copy-start.21 = (f32[1920,512]{0,1:T(8,128)}, f32[1920,512]{0,1:T(8,128)S(1)}, u32[]{:S(2)}) copy-start(f32[1920,512]{0,1:T(8,128)S(1)} %get-tuple-element.177) | copy-start | bytes 11796484
  484.4 17.9 %collective-permute-start.2 = (bf16[6,7,512]{2,1,0:T(8,128)(2,1)S(1)}, bf16[6,7,512]{2,1,0:T(8,128)(2,1)S(1)}, u32[]{:S(2)}, u32[]{:S(2)}) collective-permute-start(bf16[6,7,512]{2,1,0:T(8,128)(2,1)S(1)} %get-tuple-element.135), channel_id=1, source_target_pairs={{0,8},{8,16},{16,24},{1,9},{9,17},{17,25},{2,10},{10,18},{18,26},{... | collective-permute-start | bytes 129032 | tf_op jit(solution)/shard_map/ppermute | solution.py:27
  489.0 13.4 %collective-permute-start.3 = (bf16[6,7,512]{2,1,0:T(8,128)(2,1)S(1)}, bf16[6,7,512]{2,1,0:T(8,128)(2,1)S(1)}, u32[]{:S(2)}, u32[]{:S(2)}) collective-permute-start(bf16[6,7,512]{2,1,0:T(8,128)(2,1)S(1)} %get-tuple-element.136), channel_id=1, source_target_pairs={{8,0},{16,8},{24,16},{9,1},{17,9},{25,17},{10,2},{18,10},{26,18},{... | collective-permute-start | bytes 129032 | tf_op jit(solution)/shard_map/ppermute | solution.py:30
  550.2 40.1 %all-to-all-start.2 = ((bf16[6,320,512]{1,0,2:T(8,128)(2,1)}), bf16[6,320,512]{1,0,2:T(8,128)(2,1)}, u32[]{:S(2)}, u32[]{:S(2)}) async-start(bf16[6,320,512]{1,0,2:T(8,128)(2,1)} %copy.211), calls=%async_computation.2 | async-start | bytes 6291456 | tf_op jit(solution)/shard_map/all_to_all | solution.py:296
  648.6 39.8 %all-to-all-start.3 = ((bf16[6,1280,128]{2,0,1:T(8,128)(2,1)}), bf16[6,1280,128]{2,0,1:T(8,128)(2,1)S(1)}, u32[]{:S(2)}, u32[]{:S(2)}) async-start(bf16[6,1280,128]{2,0,1:T(8,128)(2,1)} %copy.215), calls=%async_computation.3 | async-start | bytes 5242880 | tf_op jit(solution)/shard_map/all_to_all | solution.py:302
  652.4 266.6 %reduce-scatter.6.cloned.1.call-start = ((), (), s32[]{:S(2)}) async-start(), calls=%async_computation.9 | async-start | bytes 12976128 | tf_op jit(solution)/shard_map/reduce_scatter | solution.py:339
  798.0 121.1 %copy-start.29 = (bf16[1920,512]{1,0:T(8,128)(2,1)S(1)}, bf16[1920,512]{1,0:T(8,128)(2,1)}, u32[]{:S(2)}) copy-start(bf16[1920,512]{1,0:T(8,128)(2,1)} %copy-done.28) | copy-start | bytes 5898244
  798.0 152.3 %reduce-scatter.8.cloned.1.call-start = ((), (), s32[]{:S(2)}) async-start(), calls=%async_computation.10 | async-start | bytes 1802240 | tf_op jit(solution)/shard_map/reduce_scatter | solution.py:343
  919.0 27.2 %copy-start.140 = (f32[512]{0:T(512)S(1)}, f32[512]{0:T(512)}, u32[]{:S(2)}) copy-start(f32[512]{0:T(512)} %get-tuple-element.74) | copy-start | bytes 6148
  919.0 27.2 %copy-start.141 = (f32[512]{0:T(512)S(1)}, f32[512]{0:T(512)}, u32[]{:S(2)}) copy-start(f32[512]{0:T(512)} %get-tuple-element.78) | copy-start | bytes 6148
  919.0 27.2 %copy-start.144 = (f32[512]{0:T(512)S(1)}, f32[512]{0:T(512)}, u32[]{:S(2)}) copy-start(f32[512]{0:T(512)} %get-tuple-element.80) | copy-start | bytes 6148
  919.0 27.2 %copy-start.145 = (f32[512]{0:T(512)S(1)}, f32[512]{0:T(512)}, u32[]{:S(2)}) copy-start(f32[512]{0:T(512)} %get-tuple-element.82) | copy-start | bytes 6148
  919.0 78.8 %reduce-scatter.10.cloned.1.call-start = ((), (), s32[]{:S(2)}) async-start(), calls=%async_computation.12 | async-start | bytes 163840
  947.1 84.5 %all-gather.8.cloned.1.call-start = ((), (), s32[]{:S(2)}) async-start(), calls=%async_computation.11 | async-start | bytes 3244032 | tf_op jit(solution)/shard_map/all_gather | solution.py:351
  992.2 35.9 %copy-start.138 = (f32[2,32]{1,0:T(2,128)S(1)}, f32[2,32]{1,0:T(2,128)}, u32[]{:S(2)}) copy-start(f32[2,32]{1,0:T(2,128)} %param.22) | copy-start | bytes 772
  992.2 38.4 %copy-start.55 = (bf16[22,32,256]{2,1,0:T(8,128)(2,1)S(1)}, bf16[22,32,256]{2,1,0:T(8,128)(2,1)}, u32[]{:S(2)}) copy-start(bf16[22,32,256]{2,1,0:T(8,128)(2,1)} %reduce-scatter.8.cloned.1.call-done) | copy-start | bytes 1081348
  997.8 37.1 %copy-start.56 = (f32[22,32,256]{2,1,0:T(8,128)S(1)}, f32[22,32,256]{2,1,0:T(8,128)}, u32[]{:S(2)}) copy-start(f32[22,32,256]{2,1,0:T(8,128)} %param.16) | copy-start | bytes 2162692
  (135 other events, 778.9 us)
Sparse Core Ops, SparseCore 0:
  10.3 38.8 all-gather.3
  51.0 112.6 all-gather.5
  798.1 120.7 reduce-scatter.5
  921.7 28.4 reduce-scatter.7
  953.1 23.8 reduce-scatter.9
  978.4 36.6 all-gather.7
where the time goes:
time: 1060 us; the launch traced here: 1050 us
  matrix products  293 us (28%)
  waiting for transfers between devices  268 us (25%)
  local copies, waits for them, and re-layouts  222 us (21%)
  other arithmetic  194 us (18%)
  blocking collectives  29.4 us (3%)
  starting transfers between devices  29.2 us (3%)
  between operations  16.4 us (2%)
    reduce_scatter x1, waiting for transfers between devices, body(): lax.psum_scatter(grad_stack.astype(jnp.bfloat16), 'rows', scatter_dimensi...  121 us
    dot_general x8, matrix products, inner_cols(): lax.dot_general(first, second, (((1,), (1,)), ((), ())), preferred_elemen...  68.7 us
    unnamed x327, local copies, waits for them, and re-layouts  55 us
    all_gather x1, waiting for transfers between devices, body(): block_stack = lax.all_gather(partial_stack, 'tm', axis=0, tiled=True)  52.3 us
    dot_general x2, matrix products, conv_local(): jnp.einsum('rck,kt->rtc', output_hat, inverse_table, precision=three_pass)  49.9 us
    dot_general x8, matrix products, inner_rows(): lax.dot_general(first, second, (((0,), (0,)), ((), ())), preferred_elemen...  46.5 us
    all_gather x1, waiting for transfers between devices, body(): partial_stack = lax.all_gather(copy_part, 'rows', axis=1, tiled=True)  39.7 us
    dot_general x8, matrix products, matmul(): return jnp.dot(first, second, preferred_element_type=jnp.float32)  38.7 us
  transfers between devices with their start and end apart: 14, of which 7 were waited for; matrix products, arithmetic and copies ran while one was open for 25% of the time, Pallas kernels for 0%

commit v1 on v0

v1 whole, which is shorter than its diff:
```python
from functools import partial
import math

import jax
import jax.numpy as jnp
from jax import lax
from jax.experimental import pallas as pl
from jax.experimental.pallas import tpu as pltpu
from jax.sharding import PartitionSpec as P

D = 512
FF = 2048
NST = 32
KW = 15
BS = 256
HEADS = 8
HALF = 64
LANES = 128
SUB = 16
PAD = 8
VMEM_BYTES = 60 * 1024 * 1024

rate_blocks = 0.1
rate_small = 0.5
bf16 = jnp.bfloat16
f32 = jnp.float32


def shape(dims, dtype=f32):
    return jax.ShapeDtypeStruct(dims, dtype)


def mm(a, b):
    return jnp.dot(a, b, preferred_element_type=f32)


def mm_nt(a, b):
    return lax.dot_general(a, b, (((1,), (1,)), ((), ())), preferred_element_type=f32)


def mm_tn(a, b):
    return lax.dot_general(a, b, (((0,), (0,)), ((), ())), preferred_element_type=f32)


def sigmoid(v):
    return 0.5 * jnp.tanh(0.5 * v) + 0.5


def norm(v):
    center = v - jnp.mean(v, axis=-1, keepdims=True)
    spread = jnp.mean(center * center, axis=-1, keepdims=True)
    inv = lax.rsqrt(spread + 1e-05)
    return center * inv, inv


def norm_back(hat, inv, scale, incoming):
    scaled = incoming * scale
    mean_one = jnp.mean(scaled, axis=-1, keepdims=True)
    mean_two = jnp.mean(scaled * hat, axis=-1, keepdims=True)
    return inv * (scaled - mean_one - hat * mean_two)


def fold8(v):
    return jnp.sum(v.reshape(-1, 8, v.shape[-1]), axis=0)


def load_matrices(stack, plan, sem):
    copies = []
    for first, dst in plan:
        down, across = dst.shape[0] // BS, dst.shape[1] // BS
        for i in range(down):
            for j in range(across):
                copies.append(
                    pltpu.make_async_copy(
                        stack.at[first + i * across + j],
                        dst.at[pl.ds(i * BS, BS), pl.ds(j * BS, BS)],
                        sem,
                    )
                )
    for copy in copies:
        copy.start()
    for copy in copies:
        copy.wait()


def store_blocks(acc, out, scaling, transposed=False):
    rows, cols = acc.shape
    if transposed:
        for i in range(cols // BS):
            for j in range(rows // BS):
                part = acc[pl.ds(j * BS, BS), pl.ds(i * BS, BS)] * scaling
                out[i * (rows // BS) + j] = part.T.astype(bf16)
    else:
        for i in range(rows // BS):
            for j in range(cols // BS):
                part = acc[pl.ds(i * BS, BS), pl.ds(j * BS, BS)] * scaling
                out[i * (cols // BS) + j] = part.astype(bf16)


def head_mask():
    row = lax.broadcasted_iota(jnp.int32, (HEADS * NST, D), 0) // NST
    col = lax.broadcasted_iota(jnp.int32, (HEADS * NST, D), 1) // HALF
    return (row == col).astype(f32)


def spread_heads(v, mask):
    return (jnp.concatenate([v] * HEADS, axis=0) * mask).astype(bf16)


def local_states(table, v, out):
    first = lax.broadcasted_iota(jnp.int32, (NST, LANES), 1) < HALF
    for g in range(D // LANES):
        both = mm(table[pl.ds(2 * NST * g, 2 * NST), :], v[:, g * LANES : (g + 1) * LANES])
        out[0, :, pl.ds(g * LANES, LANES)] = jnp.where(first, both[:NST], both[NST:])


def ffa_forward_kernel(feat, small, stack, mfin, x1_o, inner_o, act_o, u_o, f_o, wi, wo, wu, sem):
    @pl.when(pl.program_id(0) == 0)
    def _():
        ffn, mix = D // BS * (FF // BS), (D // BS) ** 2
        load_matrices(stack, ((0, wi), (ffn, wo), (4 * ffn, wu)), sem)

    x0 = feat[0].astype(f32)
    hat, unused = norm(x0)
    inner = mm((hat * small[0:1]).astype(bf16), wi[...])
    act = (inner * sigmoid(inner)).astype(bf16)
    inner_o[0] = inner.astype(bf16)
    act_o[0] = act
    x1 = x0 + 0.5 * mm(act, wo[...])
    x1_o[0] = x1
    hat, unused = norm(x1)
    u = mm((hat * small[1:2]).astype(bf16), wu[...]).astype(bf16)
    u_o[0] = u
    local_states(mfin, u, f_o)


def pack_heads(ref, rows):
    first = lax.broadcasted_iota(jnp.int32, (ref.shape[1], LANES), 1) < HALF
    low, high = [], []
    for p in range(rows // 2):
        a, b = ref[2 * p].astype(f32), ref[2 * p + 1].astype(f32)
        low.append(jnp.where(first, a, pltpu.roll(b, HALF, 1)).astype(bf16))
        high.append(jnp.where(first, pltpu.roll(a, HALF, 1), b).astype(bf16))
    return jnp.concatenate(low, axis=1), jnp.concatenate(high, axis=1)


def pack_params(v, rows):
    first = lax.broadcasted_iota(jnp.int32, v.shape, 1) < HALF
    rolled = pltpu.roll(v, HALF, 1)
    low = jnp.where(first, v, rolled)
    high = jnp.where(first, rolled, v)
    return (
        jnp.concatenate([low] * (rows // 2), axis=1),
        jnp.concatenate([high] * (rows // 2), axis=1),
    )


def unpack_pair(low, high, p):
    low = low[:, p * LANES : (p + 1) * LANES]
    high = high[:, p * LANES : (p + 1) * LANES]
    first = lax.broadcasted_iota(jnp.int32, low.shape, 1) < HALF
    return (
        jnp.where(first, low, pltpu.roll(high, HALF, 1)),
        jnp.where(first, pltpu.roll(low, HALF, 1), high),
    )


def conv_forward_kernel(u, m_tab, p_tab, coup, taps, y_o, pad):
    rows, frames = u.shape[0], u.shape[1]
    sub = frames // SUB
    coup_both = pack_params(coup[...], rows)
    packed = pack_heads(u, rows)
    results = []
    for h in range(2):
        states = mm(m_tab[h], packed[h])
        scaled = (states.reshape(sub, NST, -1) * coup_both[h][None]).reshape(states.shape)
        results.append(mm(p_tab[h], scaled.astype(bf16)))
    for p in range(rows // 2):
        one, two = unpack_pair(results[0], results[1], p)
        y_o[2 * p] = one
        y_o[2 * p + 1] = two
    pad[0:SUB] = jnp.zeros((SUB, LANES), f32)
    chunk = frames // 5
    for i in range(rows):
        pad[pl.ds(SUB, frames)] = u[i].astype(f32)
        for r in range(0, frames, chunk):
            acc = y_o[i, pl.ds(r, chunk)].reshape(-1, SUB, LANES)
            for d in range(SUB):
                piece = pad[pl.ds(SUB + r - d, chunk)].reshape(-1, SUB, LANES)
                acc = acc + piece * taps[d][None]
            y_o[i, pl.ds(r, chunk)] = acc.reshape(chunk, LANES)


def mixer_out_kernel(
    y, zin, x1, small, stack, pfull, ys_o, gated_o, x2_o, pw_o, g_o, wo, wp, mask, sem
):
    @pl.when(pl.program_id(0) == 0)
    def _():
        ffn, mix = D // BS * (FF // BS), (D // BS) ** 2
        load_matrices(stack, ((4 * ffn + mix, wo), (4 * ffn + 3 * mix, wp)), sem)
        mask[...] = head_mask()

    ys = (y[0] + mm(pfull[...], spread_heads(zin[0], mask[...]))).astype(bf16)
    ys_o[0] = ys
    gated = mm(ys, wo[...])
    gated_o[0] = gated.astype(bf16)
    x2 = x1[0] + gated[:, :D] * sigmoid(gated[:, D:])
    x2_o[0] = x2
    hat, unused = norm(x2)
    pw = mm((hat * small[2:3]).astype(bf16), wp[...])
    pw_o[0] = pw.astype(bf16)
    g_o[0] = (pw[:, :D] * sigmoid(pw[:, D:])).astype(bf16)


def fill_pad(pad, low, body, high):
    frames = body.shape[0]
    for g in range(D // LANES):
        lanes = slice(g * LANES, (g + 1) * LANES)
        pad[g, 0:PAD] = low[:, lanes].astype(f32)
        pad[g, pl.ds(PAD, frames)] = body[:, lanes].astype(f32)
        pad[g, pl.ds(PAD + frames, PAD)] = high[:, lanes].astype(f32)


def ffb_kernel(
    g, low, high, x2, cot, small, stack, scale,
    out_o, dx3_o, dq_o, gin_o, gout_o, gq_o, gain_o,
    wi, wo, wq, acc_in, acc_out, acc_q, pad, q_s, sem,
):
    step = pl.program_id(0)
    frames = g.shape[1]

    @pl.when(step == 0)
    def _():
        ffn, mix = D // BS * (FF // BS), (D // BS) ** 2
        load_matrices(stack, ((2 * ffn, wi), (3 * ffn, wo), (4 * ffn + 5 * mix, wq)), sem)
        acc_in[...] = jnp.zeros_like(acc_in)
        acc_out[...] = jnp.zeros_like(acc_out)
        acc_q[...] = jnp.zeros_like(acc_q)
        gain_o[...] = jnp.zeros_like(gain_o)

    fill_pad(pad, low[0], g[0], high[0])
    chunk = frames // 5
    for c in range(D // LANES):
        lanes = slice(c * LANES, (c + 1) * LANES)
        for r in range(0, frames, chunk):
            acc = small[5:6, lanes] * pad[c, pl.ds(r + PAD - 7, chunk)]
            for j in range(1, KW):
                acc = acc + small[5 + j : 6 + j, lanes] * pad[c, pl.ds(r + j + PAD - 7, chunk)]
            q_s[pl.ds(r, chunk), lanes] = acc
    q = q_s[...]
    sig_q = sigmoid(q)
    act_q = q * sig_q
    a3 = act_q.astype(bf16)
    x3 = x2[0] + mm(a3, wq[...])
    hat3, inv3 = norm(x3)
    n3 = (hat3 * small[3:4]).astype(bf16)
    inner = mm(n3, wi[...])
    sig = sigmoid(inner)
    act = inner * sig
    b4 = act.astype(bf16)
    x4 = x3 + 0.5 * mm(b4, wo[...])
    hat4, inv4 = norm(x4)
    out_o[0] = (hat4 * small[4:5]).astype(bf16)
    c4 = cot[0].astype(f32)
    gain_o[1] += fold8(c4 * hat4)
    dx4 = norm_back(hat4, inv4, small[4:5], c4)
    dp = (0.5 * dx4).astype(bf16)
    acc_out[...] += mm_tn(dp, b4)
    dact = mm_nt(dp, wo[...])
    dinner = ((sig + act * (1.0 - sig)) * dact).astype(bf16)
    acc_in[...] += mm_tn(n3, dinner)
    dn3 = mm_nt(dinner, wi[...])
    gain_o[0] += fold8(dn3 * hat3)
    dx3 = dx4 + norm_back(hat3, inv3, small[3:4], dn3)
    dx3_o[0] = dx3
    dpq = dx3.astype(bf16)
    acc_q[...] += mm_tn(a3, dpq)
    da3 = mm_nt(dpq, wq[...])
    dq_o[0] = ((sig_q + act_q * (1.0 - sig_q)) * da3).astype(bf16)

    @pl.when(step == pl.num_programs(0) - 1)
    def _():
        store_blocks(acc_in, gin_o, scale)
        store_blocks(acc_out, gout_o, scale, transposed=True)
        store_blocks(acc_q, gq_o, scale)


def mixer_back_kernel(
    dq, dlow, dhigh, g, glow, ghigh, pw, x2, gated, ys, dx3, small, stack, pfull_t, scale,
    dx2_o, dy_o, gst_o, gp_o, go_o, gain_o, dk_o,
    wo, wp, acc_p, acc_o, dpad, gpad, dg_s, dk_s, sem,
):
    step = pl.program_id(0)
    frames = dq.shape[1]

    @pl.when(step == 0)
    def _():
        ffn, mix = D // BS * (FF // BS), (D // BS) ** 2
        load_matrices(stack, ((4 * ffn + mix, wo), (4 * ffn + 3 * mix, wp)), sem)
        acc_p[...] = jnp.zeros_like(acc_p)
        acc_o[...] = jnp.zeros_like(acc_o)
        gain_o[...] = jnp.zeros_like(gain_o)
        dk_s[...] = jnp.zeros_like(dk_s)

    fill_pad(dpad, dlow[0], dq[0], dhigh[0])
    fill_pad(gpad, glow[0], g[0], ghigh[0])
    chunk = frames // 5
    for c in range(D // LANES):
        lanes = slice(c * LANES, (c + 1) * LANES)
        for r in range(0, frames, chunk):
            here = dpad[c, pl.ds(r + PAD, chunk)]
            acc = small[5:6, lanes] * dpad[c, pl.ds(r + PAD + 7, chunk)]
            for j in range(1, KW):
                acc = acc + small[5 + j : 6 + j, lanes] * dpad[c, pl.ds(r - j + PAD + 7, chunk)]
            dg_s[pl.ds(r, chunk), lanes] = acc
            for j in range(KW):
                dk_s[j, :, lanes] += fold8(here * gpad[c, pl.ds(r + j + PAD - 7, chunk)])
    dg = dg_s[...]
    value = pw[0, :, :D].astype(f32)
    gate = sigmoid(pw[0, :, D:].astype(f32))
    dvalue = (dg * gate).astype(bf16)
    dgate = (dg * value * gate * (1.0 - gate)).astype(bf16)
    dpw = jnp.concatenate([dvalue, dgate], axis=1)
    hat2, inv2 = norm(x2[0])
    n2 = (hat2 * small[2:3]).astype(bf16)
    acc_p[...] += mm_tn(n2, dpw)
    dn2 = mm_nt(dpw, wp[...])
    gain_o[...] += fold8(dn2 * hat2)
    dx2 = dx3[0] + norm_back(hat2, inv2, small[2:3], dn2)
    dx2_o[0] = dx2
    value = gated[0, :, :D].astype(f32)
    gate = sigmoid(gated[0, :, D:].astype(f32))
    dvalue = (dx2 * gate).astype(bf16)
    dgate = (dx2 * value * gate * (1.0 - gate)).astype(bf16)
    dgated = jnp.concatenate([dvalue, dgate], axis=1)
    acc_o[...] += mm_tn(ys[0], dgated)
    dy = mm_nt(dgated, wo[...]).astype(bf16)
    dy_o[0] = dy
    local_states(pfull_t, dy, gst_o)

    @pl.when(step == pl.num_programs(0) - 1)
    def _():
        store_blocks(acc_p, gp_o, scale)
        store_blocks(acc_o, go_o, scale)
        for j in range(KW):
            dk_o[j : j + 1] = jnp.sum(dk_s[j], axis=0, keepdims=True)


def conv_back_kernel(
    u, dy, m_tab, mp_tab, pt_tab, ptp_tab, mt_tab, coup, taps,
    du_o, t1_o, t2_o, fp_o, gp_o, dk_o,
    upad, dpad, acc_s,
):
    rows, frames = u.shape[0], u.shape[1]
    sub = frames // SUB
    last = (sub - 1) * NST
    coup_both = pack_params(coup[...], rows)
    u_both = pack_heads(u, rows)
    d_both = pack_heads(dy, rows)
    du, first_sum, second_sum, end_u, end_d = [], [], [], [], []
    for h in range(2):
        states = mm(m_tab[h], u_both[h])
        states_w = mm(mp_tab[h], u_both[h])
        back = mm(pt_tab[h], d_both[h])
        back_w = mm(ptp_tab[h], d_both[h])
        end_u.append(states_w[last:])
        end_d.append(back_w[last:])
        s3 = states[:last].reshape(sub - 1, NST, -1)
        b3 = back[:last].reshape(sub - 1, NST, -1)
        sw3 = states_w[:last].reshape(sub - 1, NST, -1)
        bw3 = back_w[:last].reshape(sub - 1, NST, -1)
        first_sum.append(jnp.sum(s3 * b3, axis=0))
        second_sum.append(jnp.sum(bw3 * s3 + b3 * sw3, axis=0))
        grads = (back.reshape(sub, NST, -1) * coup_both[h][None]).reshape(back.shape)
        du.append(mm(mt_tab[h], grads.astype(bf16)))
    first = lax.broadcasted_iota(jnp.int32, (NST, LANES), 1) < HALF
    for sums, out in ((first_sum, t1_o), (second_sum, t2_o)):
        both = []
        for v in sums:
            total = v[:, :LANES]
            for p in range(1, rows // 2):
                total = total + v[:, p * LANES : (p + 1) * LANES]
            both.append(total + pltpu.roll(total, HALF, 1))
        out[...] = jnp.where(first, both[0], both[1])
    for p in range(rows // 2):
        for pair, out in ((du, du_o), (end_u, fp_o), (end_d, gp_o)):
            one, two = unpack_pair(pair[0], pair[1], p)
            out[2 * p] = one
            out[2 * p + 1] = two
    chunk = frames // 5
    upad[0:SUB] = jnp.zeros((SUB, LANES), f32)
    dpad[pl.ds(frames, SUB)] = jnp.zeros((SUB, LANES), f32)
    acc_s[...] = jnp.zeros_like(acc_s)
    for i in range(rows):
        upad[pl.ds(SUB, frames)] = u[i].astype(f32)
        dpad[pl.ds(0, frames)] = dy[i].astype(f32)
        for r in range(0, frames, chunk):
            acc = du_o[i, pl.ds(r, chunk)].reshape(-1, SUB, LANES)
            here = dpad[pl.ds(r, chunk)]
            for d in range(SUB):
                piece = dpad[pl.ds(r + d, chunk)].reshape(-1, SUB, LANES)
                acc = acc + piece * taps[d][None]
                product = (here * upad[pl.ds(SUB + r - d, chunk)]).reshape(-1, SUB, LANES)
                acc_s[d] += jnp.sum(product, axis=0)
            du_o[i, pl.ds(r, chunk)] = acc.reshape(chunk, LANES)
    place = lax.broadcasted_iota(jnp.int32, (SUB, LANES), 0)
    for d in range(SUB):
        kept = jnp.where(place >= d, acc_s[d], 0.0)
        dk_o[d : d + 1] = jnp.sum(kept, axis=0, keepdims=True)


def ffa_back_kernel(
    du_loc, lam, x1, feat, inner_r, act_r, dx2, small, stack, mfin_t, scale,
    dx0_o, gin_o, gout_o, gu_o, gain_o,
    wi, wo, wu, acc_in, acc_out, acc_u, mask, sem,
):
    step = pl.program_id(0)

    @pl.when(step == 0)
    def _():
        ffn, mix = D // BS * (FF // BS), (D // BS) ** 2
        load_matrices(stack, ((0, wi), (ffn, wo), (4 * ffn, wu)), sem)
        mask[...] = head_mask()
        acc_in[...] = jnp.zeros_like(acc_in)
        acc_out[...] = jnp.zeros_like(acc_out)
        acc_u[...] = jnp.zeros_like(acc_u)
        gain_o[...] = jnp.zeros_like(gain_o)

    du = (du_loc[0] + mm(mfin_t[...], spread_heads(lam[0], mask[...]))).astype(bf16)
    hat1, inv1 = norm(x1[0])
    n1 = (hat1 * small[1:2]).astype(bf16)
    acc_u[...] += mm_tn(n1, du)
    dn1 = mm_nt(du, wu[...])
    gain_o[1] += fold8(dn1 * hat1)
    dx1 = dx2[0] + norm_back(hat1, inv1, small[1:2], dn1)
    dp = (0.5 * dx1).astype(bf16)
    acc_out[...] += mm_tn(dp, act_r[0])
    dact = mm_nt(dp, wo[...])
    inner = inner_r[0].astype(f32)
    sig = sigmoid(inner)
    dinner = ((sig + inner * sig * (1.0 - sig)) * dact).astype(bf16)
    hat0, inv0 = norm(feat[0].astype(f32))
    n0 = (hat0 * small[0:1]).astype(bf16)
    acc_in[...] += mm_tn(n0, dinner)
    dn0 = mm_nt(dinner, wi[...])
    gain_o[0] += fold8(dn0 * hat0)
    dx0_o[0] = dx1 + norm_back(hat0, inv0, small[0:1], dn0)

    @pl.when(step == pl.num_programs(0) - 1)
    def _():
        store_blocks(acc_in, gin_o, scale)
        store_blocks(acc_out, gout_o, scale, transposed=True)
        store_blocks(acc_u, gu_o, scale)


def shampoo_kernel(
    pick, owned, full, left, right, lroot, rroot, master, nl_o, nr_o, nm_o, nc_o, own_o
):
    for i in range(full.shape[0]):
        whole = full[i]
        mine = owned[i]
        own_o[i] = mine.astype(f32)
        nl_o[i] = 0.5 * left[i] + 0.5 * mm_nt(mine, whole)
        columns = mm_nt(pick[...], whole).astype(bf16)
        nr_o[i] = 0.5 * right[i] + 0.5 * mm(columns, whole)
        side = mm(lroot[i].astype(bf16), whole)
        step = mm(side.astype(bf16), rroot[i].astype(bf16))
        new = master[i] - rate_blocks * step
        nm_o[i] = new
        nc_o[i] = new.astype(bf16)


def peers():
    place, row = lax.axis_index("tm"), lax.axis_index("rows")
    return place, row // 2, row % 2


def square(place):
    x, y = place % 2, place // 2
    return 2 * y + 1 - x, 2 * (1 - y) + x, 2 * (1 - y) + 1 - x


def at(place, level, core):
    return {"tm": place, "rows": level * 2 + core}


def remote(src, dst, send, recv, device):
    return pltpu.make_async_remote_copy(
        src_ref=src,
        dst_ref=dst,
        send_sem=send,
        recv_sem=recv,
        device_id=device,
        device_id_type=pl.DeviceIdType.MESH,
    )


def signal(sem, device):
    pl.semaphore_signal(sem, inc=1, device_id=device, device_id_type=pl.DeviceIdType.MESH)


def chunk_ranges(count, chunks):
    edges = [count * c // chunks for c in range(chunks + 1)]
    out = []
    for first, end in zip(edges[:-1], edges[1:]):
        middle = (first + end + 1) // 2
        out.append((first, end, middle))
    return out


def gather_kernel(
    levels, piece, pack, stack, pack_all, own_sem, pk_send, pk_recv,
    z_send, z_recv, x_send, x_recv, y_send, y_recv, c_send, c_recv,
):
    place, level, core = peers()
    count = piece.shape[0]
    xp, yp, dp = others = square(place)
    up, down = level < levels - 1, level > 0
    barrier = pltpu.get_barrier_semaphore()
    for other in (xp, yp, dp):
        signal(barrier, at(other, level, core))
    signal(barrier, at(place, level, 1 - core))

    @pl.when(up)
    def _():
        signal(barrier, at(place, level + 1, core))

    @pl.when(down)
    def _():
        signal(barrier, at(place, level - 1, core))

    below = (level + levels - 1) // levels
    above = (2 * levels - 2 - level) // levels
    pl.semaphore_wait(barrier, 4 + below + above)

    sends = []
    own = pltpu.make_async_copy(piece, stack.at[place, :, level, core], own_sem)
    own.start()
    own_pack = pltpu.make_async_copy(pack, pack_all.at[place], pk_send.at[3])
    own_pack.start()
    ranges = chunk_ranges(count, z_send.shape[0])

    def z_copy(c, side, s):
        first, end, unused = ranges[c]
        step = 1 if side == 0 else -1
        origin = level - s * step
        spot = stack.at[place, pl.ds(first, end - first), origin, core]
        src = piece.at[pl.ds(first, end - first)] if s == 0 else spot
        return remote(
            src, spot, z_send.at[c, side, s], z_recv.at[c, side, s], at(place, (level + step + levels) % levels, core)
        )

    def z_ok(side, s):
        if side == 0:
            return jnp.logical_and(level - s >= 0, level + 1 < levels)
        return jnp.logical_and(level + s < levels, level - 1 >= 0)

    def z_in(side, s):
        if side == 0:
            return level - s - 1 >= 0
        return level + s + 1 < levels

    for c in range(len(ranges)):
        for side in range(2):
            pl.when(z_ok(side, 0))(lambda c=c, side=side: z_copy(c, side, 0).start())
        if c == 0:
            for d in range(1, 4):
                copy = remote(
                    pack,
                    pack_all.at[place],
                    pk_send.at[d - 1],
                    pk_recv.at[d - 1],
                    at(others[d - 1], level, core),
                )
                copy.start()
                sends.append(copy)
    own.wait()
    own_pack.wait()

    def part(owner, first, end):
        return stack.at[owner, pl.ds(first, end - first), :, core]

    def to_x(c, i, owner, first, end):
        return remote(
            part(owner, first, end), part(owner, first, end),
            x_send.at[c, i], x_recv.at[c, i], at(xp, level, core),
        )

    def to_y(c, i, owner, first, end):
        return remote(
            part(owner, first, end), part(owner, first, end),
            y_send.at[c, i], y_recv.at[c, i], at(yp, level, core),
        )

    def to_core(c, i, owner, first, end):
        return remote(
            part(owner, first, end), part(owner, first, end),
            c_send.at[c, i], c_recv.at[c, i], at(place, level, 1 - core),
        )

    def go(copy):
        copy.start()
        sends.append(copy)
        return copy

    moved = []

    def z_phase(c):
        for s in range(levels - 1):
            for side in range(2):

                def step(c=c, side=side, s=s):
                    z_copy(c, side, s).wait_recv()
                    if s + 1 < levels - 1:
                        pl.when(z_ok(side, s + 1))(lambda: z_copy(c, side, s + 1).start())

                pl.when(z_in(side, s))(step)

    def spread(c):
        first, end, middle = ranges[c]
        out = (
            go(to_x(c, 0, place, first, middle)),
            go(to_y(c, 0, place, middle, end)),
            go(to_x(c, 1, place, middle, end)),
            go(to_y(c, 1, place, first, middle)),
        )
        moved.append(go(to_core(c, 0, place, first, end)))
        return out

    def forward(c, copies):
        first, end, middle = ranges[c]
        copies[0].wait_recv()
        y_in = go(to_y(c, 2, xp, first, middle))
        copies[1].wait_recv()
        x_in = go(to_x(c, 2, yp, middle, end))
        moved.append(go(to_core(c, 1, xp, first, middle)))
        moved.append(go(to_core(c, 2, yp, middle, end)))
        copies[2].wait_recv()
        moved.append(go(to_core(c, 3, xp, middle, end)))
        copies[3].wait_recv()
        moved.append(go(to_core(c, 4, yp, first, middle)))
        return y_in, x_in

    def finish(c, copies):
        first, end, middle = ranges[c]
        copies[0].wait_recv()
        moved.append(go(to_core(c, 5, dp, first, middle)))
        copies[1].wait_recv()
        moved.append(go(to_core(c, 6, dp, middle, end)))

    out = {}
    for c in range(len(ranges)):
        z_phase(c)
        mine = spread(c)
        if c >= 1:
            out[c - 1] = forward(c - 1, out[c - 1])
        out[c] = mine
        if c >= 2:
            finish(c - 2, out[c - 2])
    last = len(ranges) - 1
    out[last] = forward(last, out[last])
    for c in range(max(last - 1, 0), last + 1):
        finish(c, out[c])
    for copy in moved:
        copy.wait_recv()
    for copy in sends[:3]:
        copy.wait_recv()
    for copy in sends:
        copy.wait_send()
    for c in range(len(ranges)):
        for side in range(2):
            for s in range(levels - 1):
                pl.when(z_ok(side, s))(lambda c=c, side=side, s=s: z_copy(c, side, s).wait_send())


def gather_weights(piece, pack, parts, devices, chunks=2):
    count, slab, cols = piece.shape
    if parts != 4:
        stack = lax.all_gather(lax.all_gather(piece, "rows", axis=1, tiled=True), "tm", axis=0)
        return stack.reshape(-1, BS, BS), lax.all_gather(pack, "tm", axis=0)
    levels = devices // 2
    dma = lambda *dims: pltpu.SemaphoreType.DMA(dims)
    stack, pack_all = pl.pallas_call(
        partial(gather_kernel, levels),
        in_specs=[ANY, ANY],
        out_specs=[ANY, ANY],
        out_shape=[
            shape((parts, count, levels, 2, slab, cols), piece.dtype),
            shape((parts,) + pack.shape, pack.dtype),
        ],
        scratch_shapes=[
            pltpu.SemaphoreType.DMA,
            dma(4), dma(3),
            dma(chunks, 2, levels - 1), dma(chunks, 2, levels - 1),
            dma(chunks, 3), dma(chunks, 3),
            dma(chunks, 3), dma(chunks, 3),
            dma(chunks, 7), dma(chunks, 7),
        ],
        compiler_params=pltpu.CompilerParams(
            collective_id=1, has_side_effects=True, vmem_limit_bytes=VMEM_BYTES
        ),
        name="gather_weights",
    )(piece, pack)
    return stack.reshape(-1, BS, BS), pack_all


def reduce_kernel(
    levels, grads, small, full, owned, small_sum,
    mine, came, from_x, from_y, red, z_in, s_tm, s_core, s_z,
    load_sem, c_send, c_recv, x_send, x_recv, y_send, y_recv,
    z_send, z_recv, a_send, a_recv, f_send, f_recv, s_send, s_recv, put_sem,
):
    place, level, core = peers()
    count = grads.shape[1]
    xp, yp, dp = others = square(place)
    barrier = pltpu.get_barrier_semaphore()
    for other in (xp, yp, dp):
        signal(barrier, at(other, level, core))
    signal(barrier, at(place, level, 1 - core))
    for d in range(1, levels):
        signal(barrier, at(place, (level + d) % levels, core))
    pl.semaphore_wait(barrier, 4 + levels - 1)
    ranges = chunk_ranges(count, c_send.shape[0])
    sends = []

    def go(copy):
        copy.start()
        sends.append(copy)
        return copy

    def over(ref, first, end):
        return ref.at[:, pl.ds(first, end - first)]

    loads, core_in = [], []
    for c, (first, end, unused) in enumerate(ranges):
        core_in.append(
            go(
                remote(
                    over(grads, first, end).at[:, :, :, 1 - core],
                    over(came, first, end),
                    c_send.at[c],
                    c_recv.at[c],
                    at(place, level, 1 - core),
                )
            )
        )
        load = pltpu.make_async_copy(
            over(grads, first, end).at[:, :, :, core], over(mine, first, end), load_sem.at[c]
        )
        load.start()
        loads.append(load)

    small_in = []
    for d in range(1, 4):
        small_in.append(
            go(
                remote(
                    small.at[others[d - 1]], s_tm.at[d - 1], s_send.at[d - 1], s_recv.at[d - 1],
                    at(others[d - 1], level, core),
                )
            )
        )
    for copy in small_in:
        copy.wait_recv()
    s_core[0] = small[place] + (s_tm[0] + s_tm[1]) + s_tm[2]
    swap = go(
        remote(s_core.at[0], s_core.at[1], s_send.at[3], s_recv.at[3], at(place, level, 1 - core))
    )

    def add_core(owner, first, end):
        def one(k, carry):
            total = mine[owner, k].astype(f32) + came[owner, k].astype(f32)
            mine[owner, k] = total.astype(bf16)
            return carry

        lax.fori_loop(first, end, one, 0)

    def add_into(owner, ref, slot, first, end):
        def one(k, carry):
            total = mine[owner, k].astype(f32) + ref[slot, k].astype(f32)
            mine[owner, k] = total.astype(bf16)
            return carry

        lax.fori_loop(first, end, one, 0)

    def to_x(c, i, owner, slot, first, end):
        n = pl.ds(first, end - first)
        return go(
            remote(
                mine.at[owner, n], from_x.at[slot, n], x_send.at[c, i], x_recv.at[c, i],
                at(xp, level, core),
            )
        )

    def to_y(c, i, owner, slot, first, end):
        n = pl.ds(first, end - first)
        return go(
            remote(
                mine.at[owner, n], from_y.at[slot, n], y_send.at[c, i], y_recv.at[c, i],
                at(yp, level, core),
            )
        )

    def begin(c):
        first, end, middle = ranges[c]
        loads[c].wait()
        core_in[c].wait_recv()
        add_core(dp, first, end)
        x_one = to_x(c, 0, dp, 0, first, middle)
        y_one = to_y(c, 0, dp, 0, middle, end)
        add_core(xp, first, end)
        x_two = to_x(c, 1, xp, 1, first, middle)
        add_core(yp, first, end)
        y_two = to_y(c, 1, yp, 1, middle, end)
        add_core(place, first, end)
        return x_one, y_one, x_two, y_two

    def second(c, copies):
        first, end, middle = ranges[c]
        copies[0].wait_recv()
        add_into(yp, from_x, 0, first, middle)
        y_three = to_y(c, 2, yp, 1, first, middle)
        copies[1].wait_recv()
        add_into(xp, from_y, 0, middle, end)
        x_three = to_x(c, 2, xp, 1, middle, end)
        return copies[2], copies[3], x_three, y_three

    def along(c, copies):
        first, end, middle = ranges[c]
        for copy in copies:
            copy.wait_recv()

        def one(k, carry):
            total = mine[place, k].astype(f32) + from_x[1, k].astype(f32)
            red[k] = (total + from_y[1, k].astype(f32)).astype(bf16)
            return carry

        lax.fori_loop(first, end, one, 0)
        out = []
        n = pl.ds(first, end - first)
        for d in range(1, levels):
            target = (level + d) % levels
            out.append(
                go(
                    remote(
                        red.at[n, target], z_in.at[d - 1, n], z_send.at[c, d - 1],
                        z_recv.at[c, d - 1], at(place, target, core),
                    )
                )
            )
        return out

    def settle(c, copies):
        first, end, middle = ranges[c]
        for copy in copies:
            copy.wait_recv()

        def one(k, carry):
            total = red[k, level].astype(f32)
            for d in range(levels - 1):
                total = total + z_in[d, k].astype(f32)
            owned[k] = total.astype(bf16)
            return carry

        lax.fori_loop(first, end, one, 0)
        n = pl.ds(first, end - first)
        out = []
        for d in range(1, levels):
            target = (level + d) % levels
            out.append(
                go(
                    remote(
                        owned.at[n], full.at[n, level, core], a_send.at[c, d - 1],
                        a_recv.at[c, d - 1], at(place, target, core),
                    )
                )
            )
        put = pltpu.make_async_copy(owned.at[n], full.at[n, level, core], put_sem.at[c])
        put.start()
        sibling = go(
            remote(
                owned.at[n], full.at[n, level, core], f_send.at[c, 0], f_recv.at[c, 0],
                at(place, level, 1 - core),
            )
        )
        return out, put, [sibling]

    def share(c, state):
        first, end, middle = ranges[c]
        n = pl.ds(first, end - first)
        copies, put, passed = state
        for d in range(1, levels):
            copies[d - 1].wait_recv()
            source = (level + levels - d) % levels
            passed.append(
                go(
                    remote(
                        full.at[n, source, core], full.at[n, source, core], f_send.at[c, d],
                        f_recv.at[c, d], at(place, level, 1 - core),
                    )
                )
            )
        put.wait()
        return passed

    chunks = len(ranges)
    state = [begin(0)]
    swap.wait_recv()
    s_z[level] = s_core[0] + s_core[1]
    small_z = []
    for d in range(1, levels):
        target = (level + d) % levels
        small_z.append(
            go(
                remote(
                    s_z.at[level], s_z.at[level], s_send.at[3 + d], s_recv.at[3 + d],
                    at(place, target, core),
                )
            )
        )
    for c in range(1, chunks):
        state.append(begin(c))
        state[c - 1] = second(c - 1, state[c - 1])
        if c >= 2:
            state[c - 2] = along(c - 2, state[c - 2])
        if c >= 3:
            state[c - 3] = settle(c - 3, state[c - 3])
    state[chunks - 1] = second(chunks - 1, state[chunks - 1])
    for c in range(max(chunks - 2, 0), chunks):
        state[c] = along(c, state[c])
    for c in range(max(chunks - 3, 0), chunks):
        state[c] = settle(c, state[c])
    passed = []
    for c in range(chunks):
        passed += share(c, state[c])
    for copy in small_z:
        copy.wait_recv()
    total = s_z[0]
    for i in range(1, levels):
        total = total + s_z[i]
    small_sum[...] = total
    for copy in passed:
        copy.wait_recv()
    for copy in sends:
        copy.wait_send()


def reduce_grads(grads, small, parts, devices, slab, chunks=2):
    if parts != 4:
        owned = lax.psum_scatter(grads, "tm", scatter_dimension=0, tiled=True)
        owned = lax.psum_scatter(owned, "rows", scatter_dimension=1, tiled=True)
        full = lax.all_gather(owned, "rows", axis=1, tiled=True)
        small = lax.psum_scatter(small, "tm", scatter_dimension=0, tiled=True)[0]
        return full, owned, lax.psum(small, "rows")
    levels = devices // 2
    count = grads.shape[0] // parts
    grads = grads.reshape(parts, count, levels, 2, slab, BS)
    dma = lambda *dims: pltpu.SemaphoreType.DMA(dims)
    vb = lambda *dims: pltpu.VMEM(dims, bf16)
    vmem = pl.BlockSpec(memory_space=pltpu.VMEM)
    part = small.shape[1:]
    full, owned, small_sum = pl.pallas_call(
        partial(reduce_kernel, levels),
        in_specs=[ANY, vmem],
        out_specs=[ANY, vmem, vmem],
        out_shape=[
            shape((count, levels, 2, slab, BS), bf16),
            shape((count, slab, BS), bf16),
            shape(part),
        ],
        scratch_shapes=[
            vb(parts, count, levels, slab, BS), vb(parts, count, levels, slab, BS),
            vb(2, count, levels, slab, BS), vb(2, count, levels, slab, BS),
            vb(count, levels, slab, BS), vb(levels - 1, count, slab, BS),
            vm(3, *part), vm(2, *part), vm(levels, *part),
            dma(chunks), dma(chunks), dma(chunks),
            dma(chunks, 3), dma(chunks, 3), dma(chunks, 3), dma(chunks, 3),
            dma(chunks, levels - 1), dma(chunks, levels - 1),
            dma(chunks, levels - 1), dma(chunks, levels - 1),
            dma(chunks, levels), dma(chunks, levels),
            dma(3 + levels), dma(3 + levels), dma(chunks),
        ],
        compiler_params=pltpu.CompilerParams(
            collective_id=2, has_side_effects=True, vmem_limit_bytes=VMEM_BYTES
        ),
        name="reduce_grads",
    )(grads, small)
    return full.reshape(count, BS, BS), owned, small_sum


def row_spec(frames, width):
    return pl.BlockSpec((1, frames, width), lambda i: (i, 0, 0))


def whole_spec(*dims):
    return pl.BlockSpec(dims, lambda i: (0,) * len(dims))


ANY = pl.BlockSpec(memory_space=pl.ANY)
PARAMS = pltpu.CompilerParams(
    dimension_semantics=("arbitrary",), vmem_limit_bytes=VMEM_BYTES
)


def cost(flops, moved):
    return pl.CostEstimate(flops=int(flops), bytes_accessed=int(moved), transcendentals=0)


def vm(*dims, dtype=f32):
    return pltpu.VMEM(dims, dtype)


def exchange_edges(v, axis):
    count = lax.axis_size(axis)
    forward = [(i, i + 1) for i in range(count - 1)]
    backward = [(target, source) for source, target in forward]
    low = lax.ppermute(v[:, -PAD:], axis, forward)
    high = lax.ppermute(v[:, :PAD], axis, backward)
    return low, high


def body(
    features,
    cotangent,
    state_bank,
    state_source,
    master,
    left_stats,
    right_stats,
    left_root,
    right_root,
    small_params,
    decay_logs,
    state_mix,
):
    rows, frames, width = features.shape
    tokens = rows * frames
    parts = lax.axis_size("tm")
    place = lax.axis_index("tm")
    scaling = 1.0 / math.sqrt(tokens * parts * lax.axis_size("rows"))
    sub = frames // SUB
    ffn, mix = D // BS * (FF // BS), (D // BS) ** 2

    own_heads, own_channels = decay_logs.shape[0], state_mix.shape[1]
    starts_own = state_bank[state_source]
    flat = jnp.concatenate(
        [decay_logs.reshape(-1), state_mix.reshape(-1), starts_own.reshape(-1)]
    )
    cut_one = own_heads * NST
    cut_two = cut_one + 2 * own_channels * NST
    cut_three = cut_two + rows * own_channels * NST
    flat = jnp.pad(flat, (0, -cut_three % (8 * LANES))).reshape(-1, LANES)
    stack, packed = gather_weights(
        master.astype(bf16), flat, parts, lax.axis_size("rows")
    )
    packed = packed.reshape(parts, -1)
    logs = packed[:, :cut_one].reshape(HEADS, NST)
    mix_all = packed[:, cut_one:cut_two].reshape(parts, 2, own_channels, NST)
    mix_all = mix_all.transpose(1, 3, 0, 2).reshape(2, NST, D)
    starts = packed[:, cut_two:cut_three].reshape(parts, rows, own_channels, NST)
    starts = starts.transpose(1, 3, 0, 2).reshape(rows, NST, D)

    rates = jnp.exp(logs)
    rate_nc = jnp.repeat(rates.T, HALF, axis=1)
    coupling = mix_all[0] * mix_all[1]
    column = jnp.arange(sub * NST, dtype=jnp.int32)
    end_of = (column // NST + 1) * SUB
    rate_col = jnp.tile(rates, (1, sub))
    time = jnp.arange(frames, dtype=jnp.int32)
    age = end_of[:, None] - 1 - time[None, :]
    ok = age >= 0
    age_f = jnp.maximum(age, 0).astype(f32)
    m_f = jnp.where(ok, jnp.exp(-rate_col[:, :, None] * age_f), 0.0)
    m_tab = m_f.astype(bf16)
    mp_tab = (m_f * age_f).astype(bf16)
    age_t = end_of[None, :] - 1 - time[:, None]
    mt_tab = jnp.where(
        age_t >= 0, jnp.exp(-rate_col[:, None, :] * jnp.maximum(age_t, 0).astype(f32)), 0.0
    ).astype(bf16)
    since_t = (time % SUB + 1).astype(f32)
    inside = (time // SUB)[:, None] == (column // NST + 1)[None, :]
    p_tab = jnp.where(
        inside, jnp.exp(-rate_col[:, None, :] * since_t[:, None]), 0.0
    ).astype(bf16)
    inside_t = (time // SUB)[None, :] == (column // NST + 1)[:, None]
    final = (column // NST == sub - 1)[:, None]
    since = jnp.where(final, (time + 1).astype(f32)[None, :], since_t[None, :])
    pt_f = jnp.where(inside_t | final, jnp.exp(-rate_col[:, :, None] * since), 0.0)
    pt_tab = jnp.where(final, 0.0, pt_f).astype(bf16)
    ptp_tab = (pt_f * since).astype(bf16)
    flat = rates.reshape(-1)
    next_t = (time + 1).astype(f32)
    left_t = (frames - 1 - time).astype(f32)
    pfull = jnp.exp(-flat[None, :] * next_t[:, None]).astype(bf16)
    pfull_t = jnp.exp(-flat[:, None] * next_t[None, :]).astype(bf16)
    mfin = jnp.exp(-flat[:, None] * left_t[None, :]).astype(bf16)
    mfin_t = jnp.exp(-flat[None, :] * left_t[:, None]).astype(bf16)
    lag = jnp.arange(SUB, dtype=f32)
    lag_decay = jnp.exp(-rate_nc[None] * lag[:, None, None])
    kernel_lags = jnp.sum(coupling[None] * lag_decay, axis=1)
    slot = jnp.arange(SUB, dtype=jnp.int32)
    taps_f = jnp.where(slot[:, None, None] <= slot[None, :, None], kernel_lags[:, None, :], 0.0)
    taps_b = jnp.where(
        slot[:, None, None] + slot[None, :, None] < SUB, kernel_lags[:, None, :], 0.0
    )

    mat = lambda r, c: vm(r, c, dtype=bf16)
    dma = pltpu.SemaphoreType.DMA
    small_spec = whole_spec(*small_params.shape)
    state_spec = pl.BlockSpec((1, NST, D), lambda i: (i, 0, 0))
    x1, inner_a, act_a, u, ends = pl.pallas_call(
        ffa_forward_kernel,
        grid=(rows,),
        in_specs=[row_spec(frames, D), small_spec, ANY, whole_spec(HEADS * NST, frames)],
        out_specs=[
            row_spec(frames, D),
            row_spec(frames, FF),
            row_spec(frames, FF),
            row_spec(frames, D),
            state_spec,
        ],
        out_shape=[
            shape((rows, frames, D)),
            shape((rows, frames, FF), bf16),
            shape((rows, frames, FF), bf16),
            shape((rows, frames, D), bf16),
            shape((rows, NST, D)),
        ],
        scratch_shapes=[mat(D, FF), mat(FF, D), mat(D, D), dma],
        compiler_params=PARAMS,
        cost_estimate=cost(2 * tokens * D * (2 * FF + D), 30e6),
        name="ffa_forward",
    )(features, small_params, stack, mfin)

    group_spec = pl.BlockSpec((rows, frames, LANES), lambda i: (0, 0, i))
    table_spec = pl.BlockSpec((2, sub * NST, frames), lambda i: (i, 0, 0))
    table_t_spec = pl.BlockSpec((2, frames, sub * NST), lambda i: (i, 0, 0))
    coup_spec = pl.BlockSpec((NST, LANES), lambda i: (0, i))
    taps_spec = pl.BlockSpec((SUB, SUB, LANES), lambda i: (0, 0, i))
    conv_flops = 2 * HEADS * sub * NST * frames * HALF * rows
    y_loc = pl.pallas_call(
        conv_forward_kernel,
        grid=(D // LANES,),
        in_specs=[group_spec, table_spec, table_t_spec, coup_spec, taps_spec],
        out_specs=group_spec,
        out_shape=shape((rows, frames, D)),
        scratch_shapes=[vm(SUB + frames, LANES)],
        compiler_params=PARAMS,
        cost_estimate=cost(2 * conv_flops, 12e6),
        name="conv_forward",
    )(u, m_tab, p_tab, coupling, taps_f)

    span = float(frames)
    ends_all = lax.all_gather(ends.astype(bf16), "tm", axis=0, tiled=False).astype(f32)
    shard = jnp.arange(parts, dtype=jnp.int32)
    behind = place - 1 - shard
    behind_f = jnp.maximum(behind, 0).astype(f32) * span
    behind_w = jnp.where(
        (behind >= 0)[:, None, None],
        jnp.exp(-rate_nc[None] * behind_f[:, None, None]),
        0.0,
    )
    begin = place.astype(f32) * span
    begin_w = jnp.exp(-rate_nc * begin)
    came = jnp.sum(ends_all * behind_w[:, None], axis=0)
    zin = coupling * came + (mix_all[1] * begin_w) * starts

    ys, gated, x2, pw, g = pl.pallas_call(
        mixer_out_kernel,
        grid=(rows,),
        in_specs=[
            row_spec(frames, D),
            state_spec,
            row_spec(frames, D),
            small_spec,
            ANY,
            whole_spec(frames, HEADS * NST),
        ],
        out_specs=[
            row_spec(frames, D),
            row_spec(frames, 2 * D),
            row_spec(frames, D),
            row_spec(frames, 2 * D),
            row_spec(frames, D),
        ],
        out_shape=[
            shape((rows, frames, D), bf16),
            shape((rows, frames, 2 * D), bf16),
            shape((rows, frames, D)),
            shape((rows, frames, 2 * D), bf16),
            shape((rows, frames, D), bf16),
        ],
        scratch_shapes=[mat(D, 2 * D), mat(D, 2 * D), vm(HEADS * NST, D), dma],
        compiler_params=PARAMS,
        cost_estimate=cost(8 * tokens * D * D, 30e6),
        name="mixer_out",
    )(y_loc, zin, x1, small_params, stack, pfull)

    g_low, g_high = exchange_edges(g, "tm")
    edge_spec = pl.BlockSpec((1, PAD, D), lambda i: (i, 0, 0))
    layer_out, dx3, dq, grad_bi, grad_bo, grad_q, gain_b = pl.pallas_call(
        partial(ffb_call, scaling),
        grid=(rows,),
        in_specs=[
            row_spec(frames, D),
            edge_spec,
            edge_spec,
            row_spec(frames, D),
            row_spec(frames, D),
            small_spec,
            ANY,
        ],
        out_specs=[
            row_spec(frames, D),
            row_spec(frames, D),
            row_spec(frames, D),
            whole_spec(ffn, BS, BS),
            whole_spec(ffn, BS, BS),
            whole_spec(mix, BS, BS),
            whole_spec(2, 8, D),
        ],
        out_shape=[
            shape((rows, frames, D), bf16),
            shape((rows, frames, D)),
            shape((rows, frames, D), bf16),
            shape((ffn, BS, BS), bf16),
            shape((ffn, BS, BS), bf16),
            shape((mix, BS, BS), bf16),
            shape((2, 8, D)),
        ],
        scratch_shapes=[
            mat(D, FF),
            mat(FF, D),
            mat(D, D),
            vm(D, FF),
            vm(D, FF),
            vm(D, D),
            vm(D // LANES, frames + 2 * PAD, LANES),
            vm(frames, D),
            dma,
        ],
        compiler_params=PARAMS,
        cost_estimate=cost(6 * tokens * D * (2 * FF + D), 30e6),
        name="ffb",
    )(g, g_low, g_high, x2, cotangent, small_params, stack)

    d_low, d_high = exchange_edges(dq, "tm")
    dx2, dy, back_ends, grad_p, grad_o, gain_c, kernel_grads = pl.pallas_call(
        partial(mixer_back_call, scaling),
        grid=(rows,),
        in_specs=[
            row_spec(frames, D),
            edge_spec,
            edge_spec,
            row_spec(frames, D),
            edge_spec,
            edge_spec,
            row_spec(frames, 2 * D),
            row_spec(frames, D),
            row_spec(frames, 2 * D),
            row_spec(frames, D),
            row_spec(frames, D),
            small_spec,
            ANY,
            whole_spec(HEADS * NST, frames),
        ],
        out_specs=[
            row_spec(frames, D),
            row_spec(frames, D),
            state_spec,
            whole_spec(2 * mix, BS, BS),
            whole_spec(2 * mix, BS, BS),
            whole_spec(8, D),
            whole_spec(16, D),
        ],
        out_shape=[
            shape((rows, frames, D)),
            shape((rows, frames, D), bf16),
            shape((rows, NST, D)),
            shape((2 * mix, BS, BS), bf16),
            shape((2 * mix, BS, BS), bf16),
            shape((8, D)),
            shape((16, D)),
        ],
        scratch_shapes=[
            mat(D, 2 * D),
            mat(D, 2 * D),
            vm(D, 2 * D),
            vm(D, 2 * D),
            vm(D // LANES, frames + 2 * PAD, LANES),
            vm(D // LANES, frames + 2 * PAD, LANES),
            vm(frames, D),
            vm(KW, 8, D),
            dma,
        ],
        compiler_params=PARAMS,
        cost_estimate=cost(16 * tokens * D * D, 30e6),
        name="mixer_back",
    )(dq, d_low, d_high, g, g_low, g_high, pw, x2, gated, ys, dx3, small_params, stack, pfull_t)
    back_all = lax.all_gather(back_ends.astype(bf16), "tm", axis=0, tiled=False).astype(f32)
    nst_spec = pl.BlockSpec((rows, NST, LANES), lambda i: (0, 0, i))
    du_loc, t_one, t_two, ends_w, back_w, lag_grads = pl.pallas_call(
        conv_back_kernel,
        grid=(D // LANES,),
        in_specs=[group_spec, group_spec]
        + [table_spec] * 4
        + [table_t_spec, coup_spec, taps_spec],
        out_specs=[
            group_spec,
            coup_spec,
            coup_spec,
            nst_spec,
            nst_spec,
            pl.BlockSpec((SUB, LANES), lambda i: (0, i)),
        ],
        out_shape=[
            shape((rows, frames, D)),
            shape((NST, D)),
            shape((NST, D)),
            shape((rows, NST, D)),
            shape((rows, NST, D)),
            shape((SUB, D)),
        ],
        scratch_shapes=[
            vm(SUB + frames, LANES),
            vm(SUB + frames, LANES),
            vm(SUB, SUB, LANES),
        ],
        compiler_params=PARAMS,
        cost_estimate=cost(5 * conv_flops, 30e6),
        name="conv_back",
    )(u, dy, m_tab, mp_tab, pt_tab, ptp_tab, mt_tab, coupling, taps_b)

    ahead = shard - place - 1
    ahead_f = jnp.maximum(ahead, 0).astype(f32) * span
    ahead_w = jnp.where(
        (ahead >= 0)[:, None, None],
        jnp.exp(-rate_nc[None] * ahead_f[:, None, None]),
        0.0,
    )
    later = jnp.sum(back_all * ahead_w[:, None], axis=0)
    lam = coupling * later

    grad_zero, grad_ai, grad_ao, grad_u, gain_a = pl.pallas_call(
        partial(ffa_back_call, scaling),
        grid=(rows,),
        in_specs=[
            row_spec(frames, D),
            state_spec,
            row_spec(frames, D),
            row_spec(frames, D),
            row_spec(frames, FF),
            row_spec(frames, FF),
            row_spec(frames, D),
            small_spec,
            ANY,
            whole_spec(frames, HEADS * NST),
        ],
        out_specs=[
            row_spec(frames, D),
            whole_spec(ffn, BS, BS),
            whole_spec(ffn, BS, BS),
            whole_spec(mix, BS, BS),
            whole_spec(2, 8, D),
        ],
        out_shape=[
            shape((rows, frames, D)),
            shape((ffn, BS, BS), bf16),
            shape((ffn, BS, BS), bf16),
            shape((mix, BS, BS), bf16),
            shape((2, 8, D)),
        ],
        scratch_shapes=[
            mat(D, FF),
            mat(FF, D),
            mat(D, D),
            vm(D, FF),
            vm(D, FF),
            vm(D, D),
            vm(HEADS * NST, D),
            dma,
        ],
        compiler_params=PARAMS,
        cost_estimate=cost(4 * tokens * D * (2 * FF + D), 40e6),
        name="ffa_back",
    )(du_loc, lam, x1, features, inner_a, act_a, dx2, small_params, stack, mfin_t)
    grads = jnp.concatenate(
        [grad_ai, grad_ao, grad_bi, grad_bo, grad_u, grad_o, grad_p, grad_q], axis=0
    )

    lag_grad_c = jnp.sum(lag_decay * lag_grads[:, None, :], axis=0)
    lag_grad_r = jnp.sum(lag_decay * (lag[:, None] * lag_grads)[:, None, :], axis=0)
    came_w = jnp.sum(ends_all * (behind_w * behind_f[:, None, None])[:, None], axis=0)
    d_coup = t_one + lag_grad_c + jnp.sum(back_ends * came, axis=0)
    d_first = d_coup * mix_all[1]
    start_back = jnp.sum(starts * back_ends, axis=0) * begin_w
    d_second = d_coup * mix_all[0] + start_back
    d_rate = coupling * (
        t_two
        + lag_grad_r
        + jnp.sum(back_w * came + back_ends * came_w + later * ends_w, axis=0)
    )
    d_rate = d_rate + mix_all[1] * (
        begin * start_back + begin_w * jnp.sum(starts * back_w, axis=0)
    )
    d_logs = -jnp.sum(d_rate.reshape(NST, HEADS, HALF), axis=2).T * rates
    small_grads = jnp.concatenate(
        [
            jnp.sum(gain_a, axis=1),
            jnp.sum(gain_c, axis=0, keepdims=True),
            jnp.sum(gain_b, axis=1),
            kernel_grads[:KW],
        ],
        axis=0,
    )
    own = place * own_channels
    lanes_own = lambda v: lax.dynamic_slice_in_dim(v, own, own_channels, v.ndim - 1)
    stacked = jnp.concatenate([small_grads, d_first, d_second], axis=0) * scaling
    stacked = stacked.reshape(-1, parts, own_channels).transpose(1, 0, 2)
    logs_row = jnp.pad(
        (d_logs * scaling).reshape(parts, 1, own_heads * NST),
        ((0, 0), (0, 0), (0, own_channels - own_heads * NST)),
    )
    stacked = jnp.concatenate([stacked, logs_row], axis=1)
    stacked = jnp.pad(stacked, ((0, 0), (0, -stacked.shape[1] % 8), (0, 0)))
    full_grad, owned, sums = reduce_grads(
        grads, stacked, parts, lax.axis_size("rows"), master.shape[1]
    )
    count_small = small_params.shape[0]
    small_sum = sums[:count_small]
    mix_sum = sums[count_small : count_small + 2 * NST]
    mix_sum = mix_sum.reshape(2, NST, own_channels).transpose(0, 2, 1)
    decay_sum = sums[count_small + 2 * NST, : own_heads * NST].reshape(own_heads, NST)
    new_small = lanes_own(small_params) - rate_small * small_sum
    new_decay = decay_logs - rate_small * decay_sum
    new_mix = state_mix - rate_small * mix_sum

    shard_w = jnp.exp(-lanes_own(rate_nc)[None] * (shard.astype(f32) * span)[:, None, None])
    start_grad = jnp.sum(lanes_own(back_all) * shard_w[:, None], axis=0) * lanes_own(mix_all[1])
    start_grad = start_grad.transpose(0, 2, 1)
    chosen = (state_source[None, :] == jnp.arange(rows, dtype=jnp.int32)[:, None]).astype(f32)
    grad_state = jnp.sum(chosen[:, :, None, None] * start_grad[None], axis=1)

    count, slice_rows = owned.shape[0], owned.shape[1]
    mine = lax.axis_index("rows") * slice_rows
    pick = (
        jnp.arange(slice_rows, dtype=jnp.int32)[:, None] + mine
        == jnp.arange(BS, dtype=jnp.int32)[None, :]
    ).astype(bf16)
    group = 11 if count % 11 == 0 else 1
    part_spec = pl.BlockSpec((group, slice_rows, BS), lambda i: (i, 0, 0))
    full_spec = pl.BlockSpec((group, BS, BS), lambda i: (i, 0, 0))
    new_left, new_right, new_master, new_copy, grad_blocks = pl.pallas_call(
        shampoo_kernel,
        grid=(count // group,),
        in_specs=[
            whole_spec(slice_rows, BS),
            part_spec,
            full_spec,
            part_spec,
            part_spec,
            part_spec,
            full_spec,
            part_spec,
        ],
        out_specs=[part_spec] * 5,
        out_shape=[
            shape(owned.shape),
            shape(owned.shape),
            shape(owned.shape),
            shape(owned.shape, bf16),
            shape(owned.shape),
        ],
        compiler_params=PARAMS,
        name="shampoo",
    )(pick, owned, full_grad, left_stats, right_stats, left_root, right_root, master)
    return (
        layer_out,
        grad_zero,
        grad_state,
        grad_blocks,
        new_left,
        new_right,
        new_master,
        new_copy,
        small_sum,
        new_small,
        decay_sum,
        mix_sum,
        new_decay,
        new_mix,
    )


def ffb_call(scaling, *refs):
    ffb_kernel(*refs[:7], scaling, *refs[7:])


def mixer_back_call(scaling, *refs):
    mixer_back_kernel(*refs[:14], scaling, *refs[14:])


def ffa_back_call(scaling, *refs):
    ffa_back_kernel(*refs[:10], scaling, *refs[10:])


def solution(mesh):
    return jax.shard_map(
        body,
        mesh=mesh,
        in_specs=(
            P("rows", "tm", None),
            P("rows", "tm", None),
            P("rows", "tm", None),
            P("rows"),
            P("tm", "rows", None),
            P("tm", "rows", None),
            P("tm", "rows", None),
            P("tm", "rows", None),
            P("tm", None, None),
            P(),
            P("tm", None),
            P(None, "tm", None),
        ),
        out_specs=(
            P("rows", "tm", None),
            P("rows", "tm", None),
            P("rows", "tm", None),
            P("tm", "rows", None),
            P("tm", "rows", None),
            P("tm", "rows", None),
            P("tm", "rows", None),
            P("tm", "rows", None),
            P(None, "tm"),
            P(None, "tm"),
            P("tm", None),
            P(None, "tm", None),
            P("tm", None),
            P(None, "tm", None),
        ),
        check_vma=False,
    )
```

time: 1060 us -> 532 us (0.50)
  Pallas kernels: 0 us -> 417 us
  matrix products: 293 us -> 0 us
  waiting for transfers between devices: 268 us -> 6.9 us
  local copies, waits for them, and re-layouts: 222 us -> 26.7 us
  other arithmetic: 194 us -> 39 us
  starting transfers between devices: 29.2 us -> 10.1 us
  between operations: 16.4 us -> 1.54 us
    pallas_call x0 -> x10, Pallas kernels: none -> 417 us  [the longest x1 115 us: reduce_grads(): pl.pallas_call(partial(reduce_kernel, levels), in_specs=[ANY, vmem], out_...]
    dot_general x42 -> x0, matrix products: 293 us -> none  [the longest x8 68.7 us: inner_cols(): lax.dot_general(first, second, (((1,), (1,)), ((), ())), preferred_elemen...]
    reduce_scatter x2 -> x0, waiting for transfers between devices: 124 us -> none  [the longest x1 121 us: body(): lax.psum_scatter(grad_stack.astype(jnp.bfloat16), 'rows', scatter_dimensi...]
    all_gather x3 -> x0, waiting for transfers between devices: 92 us -> none  [the longest x1 52.3 us: body(): block_stack = lax.all_gather(partial_stack, 'tm', axis=0, tiled=True)]
    reshape x23 -> x9, local copies, waits for them, and re-layouts: 64.6 us -> 2.69 us  [the longest x1 0.76 us: body(): decay_logs.reshape(-1)]
    all_to_all x4 -> x0, waiting for transfers between devices: 52.2 us -> none  [the longest x1 24.2 us: body(): lax.all_to_all(channel_out.astype(jnp.bfloat16), 'tm', split_axis=1, conc...]
    reduce_sum x16 -> x11, other arithmetic: 51.8 us -> 7.59 us  [the longest x1 2.22 us: body(): d_coup = t_one + lag_grad_c + jnp.sum(back_ends * came, axis=0)]
    mul x8 -> x6, other arithmetic: 44.1 us -> 2.31 us  [the longest x1 0.95 us: body(): zin = coupling * came + mix_all[1] * begin_w * starts]
  transfers between devices with their start and end apart: 14 -> 4, of which waited for: 7 -> 2; matrix products, arithmetic and copies ran while one was open for 25% -> 0% of each run, Pallas kernels for 0% -> 0%
where the time goes in v1:
time: 532 us; the launch traced here: 526 us
  Pallas kernels  417 us (78%)
  other arithmetic  39 us (7%)
  local copies, waits for them, and re-layouts  26.7 us (5%)
  blocking collectives  24.5 us (5%)
  starting transfers between devices  10.1 us (2%)
  waiting for transfers between devices  6.9 us (1%)
    pallas_call x1, Pallas kernels, reduce_grads(): pl.pallas_call(partial(reduce_kernel, levels), in_specs=[ANY, vmem], out_...  115 us
    pallas_call x1, Pallas kernels, gather_weights(): pl.pallas_call(partial(gather_kernel, levels), in_specs=[ANY, ANY], out_s...  82.5 us
    pallas_call x1, Pallas kernels, body(): pl.pallas_call(partial(ffb_call, scaling), grid=(rows,), in_specs=[row_sp...  53.6 us
    pallas_call x1, Pallas kernels, body(): pl.pallas_call(partial(ffa_back_call, scaling), grid=(rows,), in_specs=[r...  42.9 us
    pallas_call x1, Pallas kernels, body(): pl.pallas_call(partial(mixer_back_call, scaling), grid=(rows,), in_specs=...  34.2 us
    pallas_call x1, Pallas kernels, body(): pl.pallas_call(conv_back_kernel, grid=(D // LANES,), in_specs=[group_spec...  31.6 us
    pallas_call x1, Pallas kernels, body(): pl.pallas_call(ffa_forward_kernel, grid=(rows,), in_specs=[row_spec(frame...  19.1 us
    pallas_call x1, Pallas kernels, body(): pl.pallas_call(conv_forward_kernel, grid=(D // LANES,), in_specs=[group_s...  14.8 us
  transfers between devices with their start and end apart: 4, of which 2 were waited for; matrix products, arithmetic and copies ran while one was open for 0% of the time, Pallas kernels for 0%

profile of v1, /device:TPU:0, one launch (start us, length us, event | category | flops | bytes accessed | tf_op | source)
XLA Modules:
  0.0 525.8 jit_solution(18094095423739590436)
XLA Ops:
  4.9 1.9 convert_element_type.147.piece
  6.8 82.5 %gather_weights.1 = (bf16[4,22,4,2,32,256]{5,4,3,2,1,0:T(8,128)(2,1)}, f32[4,264,128]{2,1,0:T(8,128)}) custom-call(bf16[22,32,256]{2,1,0:T(8,128)(2,1)} %convert_element_type.147.piece, f32[264,128]{1,0:T(8,128)} %pad_bitcast_fusion.pack), custom_call_target="tpu_custom_call" | custom-call | tf_op jit(solution)/shard_map/gather_weights/pallas_call | solution.py:683
  89.4 1.2 copy.90
  98.0 19.1 %ffa_forward.1 = (f32[6,320,512]{2,1,0:T(8,128)}, bf16[6,320,2048]{2,1,0:T(8,128)(2,1)}, bf16[6,320,2048]{2,1,0:T(8,128)(2,1)}, bf16[6,320,512]{2,1,0:T(8,128)(2,1)}, f32[6,32,512]{2,1,0:T(8,128)}) custom-call(bf16[6,320,512]{2,1,0:T(8,128)(2,1)} %refs_3_.1, f32[20,512]{1,0:T(8,128)} %refs_7_.1, bf16[88,256,256]{2,1,0:T(8,128)(2,1)} %bitcast.45, ...), custom_call_target="tpu_custom_call" | custom-call | flops 9059696640 | bytes 30000000 | tf_op jit(solution)/shard_map/ffa_forward/pallas_call | solution.py:1111
  118.1 13.5 %all-gather = bf16[24,32,512]{2,1,0:T(8,128)(2,1)} all-gather(bf16[6,32,512]{2,1,0:T(8,128)(2,1)S(1)} %convert_element_type.154), channel_id=2, replica_groups=mesh['tm'=4,'rows'=8] {'tm'}, dimensions={0}, use_global_device_ids=true | all-gather | bytes 983040 | tf_op jit(solution)/shard_map/all_gather | solution.py:1154
  133.8 1.1 fusion.3
  137.3 1.5 fusion.2
  139.6 1.1 broadcast_select_fusion.1
  140.7 5.3 %select_convert_fusion.1 = (bf16[8,320,640]{2,1,0:T(8,128)(2,1)}, bf16[8,320,640]{2,1,0:T(8,128)(2,1)}) fusion(f32[320,640]{1,0:T(8,128)} %maximum_convert_fusion.1, f32[8,640]{1,0:T(8,128)S(1)} %neg.66, pred[320,640]{1,0:T(8,128)(4,1)S(1)} %copy-done.13, f32[320]{0:T(512)S(1)} %fusion.20, pred[320,640]{1,0:T(8,128)(4,1)S(1)} %copy-done.14), kind=kLoop, calls=%fused_computation.7 | loop fusion | flops 9830400 | bytes 7804160 | tf_op jit(solution)/shard_map/convert_element_type | solution.py:1079
  146.1 7.2 %multiply_convert_fusion = (bf16[8,640,320]{2,1,0:T(8,128)(2,1)}, bf16[8,640,320]{2,1,0:T(8,128)(2,1)}, bf16[8,640,320]{2,1,0:T(8,128)(2,1)}, bf16[8,640,320]{2,1,0:T(8,128)(2,1)}) fusion(f32[640,320]{1,0:T(8,128)S(1)} %broadcast_select_fusion, f32[8,640]{1,0:T(8,128)S(1)} %neg.66, pred[640,320]{1,0:T(8,128)(4,1)S(1)} %copy-done.12, ...), kind=kLoop, calls=%fused_computation.1 | loop fusion | flops 18022400 | bytes 15176320 | tf_op jit(solution)/shard_map/convert_element_type | solution.py:1090
  153.3 14.8 %conv_forward.1.y = f32[6,320,512]{2,1,0:T(8,128)} custom-call(bf16[6,320,512]{2,1,0:T(8,128)(2,1)} %get-tuple-element.61.u, bf16[8,640,320]{2,1,0:T(8,128)(2,1)} %get-tuple-element.140.m_tab, bf16[8,320,640]{2,1,0:T(8,128)(2,1)} %get-tuple-element.139.p_tab, f32[32,512]{1,0:T(8,128)} %copy-done.2, f32[16,16,512]{2,1,0:T(8,128)} %get-tuple-element.137.taps), custom_call_target="tpu_custom_call" | custom-call | flops 2516582400 | bytes 12000000 | tf_op jit(solution)/shard_map/conv_forward/pallas_call | solution.py:1141
  168.1 13.2 %mixer_out.1 = (bf16[6,320,512]{2,1,0:T(8,128)(2,1)}, bf16[6,320,1024]{2,1,0:T(8,128)(2,1)}, f32[6,320,512]{2,1,0:T(8,128)}, bf16[6,320,1024]{2,1,0:T(8,128)(2,1)}, bf16[6,320,512]{2,1,0:T(8,128)(2,1)}) custom-call(f32[6,320,512]{2,1,0:T(8,128)} %conv_forward.1.y, f32[6,32,512]{2,1,0:T(8,128)} %multiply_add_fusion.zin, ...), custom_call_target="tpu_custom_call" | custom-call | flops 4026531840 | bytes 30000000 | tf_op jit(solution)/shard_map/mixer_out/pallas_call | solution.py:1168
  182.1 3.0 collective-permute-start
  185.2 1.5 collective-permute-start.1
  188.1 3.0 collective-permute-done.1.refs_2_.refs_5_
  191.8 53.6 %ffb.1 = (bf16[6,320,512]{2,1,0:T(8,128)(2,1)}, f32[6,320,512]{2,1,0:T(8,128)}, bf16[6,320,512]{2,1,0:T(8,128)(2,1)}, bf16[16,256,256]{2,1,0:T(8,128)(2,1)}, bf1...) custom-call(bf16[6,320,512]{2,1,0:T(8,128)(2,1)} %get-tuple-element.64.refs_0_.refs_3_, ...), custom_call_target="tpu_custom_call" | custom-call | flops 27179089920 | bytes 30000000 | tf_op jit(solution)/shard_map/ffb/pallas_call | solution.py:1201
  246.2 4.3 collective-permute-start.2
  250.5 1.3 collective-permute-start.3
  252.6 3.9 collective-permute-done.3.refs_2_
  257.1 34.2 %mixer_back.1 = (f32[6,320,512]{2,1,0:T(8,128)}, bf16[6,320,512]{2,1,0:T(8,128)(2,1)}, f32[6,32,512]{2,1,0:T(8,128)}, bf16[8,256,256]{2,1,0:T(8,128)(2,1)}, bf16...) custom-call(bf16[6,320,512]{2,1,0:T(8,128)(2,1)} %get-tuple-element.67.refs_0_, ...), custom_call_target="tpu_custom_call" | custom-call | flops 8053063680 | bytes 30000000 | tf_op jit(solution)/shard_map/mixer_back/pallas_call | solution.py:1248
  291.3 31.6 %conv_back.1 = (f32[6,320,512]{2,1,0:T(8,128)}, f32[32,512]{1,0:T(8,128)}, f32[32,512]{1,0:T(8,128)}, f32[6,32,512]{2,1,0:T(8,128)}, f32[6,32,512]{2,1,0:T(8,128)}, /*index=5*/f32[16,512]{1,0:T(8,128)}) custom-call(bf16[6,320,512]{2,1,0:T(8,128)(2,1)} %get-tuple-element.61.u, bf16[6,320,512]{2,1,0:T(8,128)(2,1)} %get-tuple-element.72.dy, ...), custom_call_target="tpu_custom_call" | custom-call | flops 6291456000 | bytes 30000000 | tf_op jit(solution)/shard_map/conv_back/pallas_call | solution.py:1302
  324.8 11.0 %all-gather.1 = bf16[24,32,512]{2,1,0:T(8,128)(2,1)S(1)} all-gather(bf16[6,32,512]{2,1,0:T(8,128)(2,1)S(1)} %convert_element_type.166), channel_id=3, replica_groups=mesh['tm'=4,'rows'=8] {'tm'}, dimensions={0}, use_global_device_ids=true | all-gather | bytes 983040 | tf_op jit(solution)/shard_map/all_gather | solution.py:1300
  336.0 2.2 multiply_reduce_fusion.7
  338.4 42.9 %ffa_back.1 = (f32[6,320,512]{2,1,0:T(8,128)}, bf16[16,256,256]{2,1,0:T(8,128)(2,1)}, bf16[16,256,256]{2,1,0:T(8,128)(2,1)}, bf16[4,256,256]{2,1,0:T(8,128)(2,1)}, f32[2,8,512]{2,1,0:T(8,128)}) custom-call(f32[6,320,512]{2,1,0:T(8,128)} %get-tuple-element.73.refs_0_, f32[6,32,512]{2,1,0:T(8,128)} %get-tuple-element.126.refs_1_, ...), custom_call_target="tpu_custom_call" | custom-call | flops 18119393280 | bytes 40000000 | tf_op jit(solution)/shard_map/ffa_back/pallas_call | solution.py:1344
  383.7 3.3 constant_dynamic-update-slice_fusion.7
  386.9 1.4 constant_dynamic-update-slice_fusion.6
  388.4 1.5 constant_dynamic-update-slice_fusion.5
  389.9 1.5 constant_dynamic-update-slice_fusion.4
  392.3 1.0 constant_dynamic-update-slice_fusion.2
  395.2 114.9 %reduce_grads.1 = (bf16[22,4,2,32,256]{4,3,2,1,0:T(8,128)(2,1)}, bf16[22,32,256]{2,1,0:T(8,128)(2,1)}, f32[88,128]{1,0:T(8,128)}) custom-call(bf16[4,22,4,2,32,256]{5,4,3,2,1,0:T(8,128)(2,1)} %bitcast.12.grads, f32[4,88,128]{2,1,0:T(8,128)} %pad.14.small), custom_call_target="tpu_custom_call" | custom-call | tf_op jit(solution)/shard_map/reduce_grads/pallas_call | solution.py:962
  510.8 1.3 multiply_subtract_fusion.1
  515.2 10.3 %shampoo.1 = (f32[22,32,256]{2,1,0:T(8,128)}, f32[22,32,256]{2,1,0:T(8,128)}, f32[22,32,256]{2,1,0:T(8,128)}, bf16[22,32,256]{2,1,0:T(8,128)(2,1)}, f32[22,32,256]{2,1,0:T(8,128)}) custom-call(bf16[32,256]{1,0:T(8,128)(2,1)} %fusion.7.pick, bf16[22,32,256]{2,1,0:T(8,128)(2,1)} %get-tuple-element.96.owned, bf16[22,256,256]{2,1,0:T(8,128)(2,1)} %bitcast.54, ...), custom_call_target="tpu_custom_call" | custom-call | tf_op jit(solution)/shard_map/shampoo/pallas_call | solution.py:1453
  (166 shorter events, 34.0 us)
Async XLA Ops:
  96.3 38.9 %copy-start.15 = (f32[32,512]{1,0:T(8,128)}, f32[32,512]{1,0:T(8,128)S(1)}, u32[]{:S(2)}) copy-start(f32[32,512]{1,0:T(8,128)S(1)} %broadcast_in_dim_reshape.2) | copy-start | bytes 196612
  98.0 33.6 %copy-start.8 = (f32[4,24576]{1,0:T(4,128)S(1)}, f32[4,24576]{1,0:T(4,128)}, u32[]{:S(2)}) copy-start(f32[4,24576]{1,0:T(4,128)} %slice.65) | copy-start | bytes 1179652
  135.2 5.5 %copy-start.13 = (pred[320,640]{1,0:T(8,128)(4,1)S(1)}, pred[320,640]{1,0:T(8,128)(4,1)}, u32[]{:S(2)}) copy-start(pred[320,640]{1,0:T(8,128)(4,1)} %get-tuple-element.154) | copy-start | bytes 614404
  135.2 5.5 %copy-start.14 = (pred[320,640]{1,0:T(8,128)(4,1)S(1)}, pred[320,640]{1,0:T(8,128)(4,1)}, u32[]{:S(2)}) copy-start(pred[320,640]{1,0:T(8,128)(4,1)} %get-tuple-element.155) | copy-start | bytes 614404
  136.2 9.9 %copy-start.2 = (f32[32,512]{1,0:T(8,128)}, f32[32,512]{1,0:T(8,128)S(1)}, u32[]{:S(2)}) copy-start(f32[32,512]{1,0:T(8,128)S(1)} %get-tuple-element.135.coup) | copy-start | bytes 196612
  140.7 5.3 %copy-start.11 = (pred[640,320]{1,0:T(8,128)(4,1)S(1)}, pred[640,320]{1,0:T(8,128)(4,1)}, u32[]{:S(2)}) copy-start(pred[640,320]{1,0:T(8,128)(4,1)} %get-tuple-element.152) | copy-start | bytes 614404
  140.7 5.3 %copy-start.12 = (pred[640,320]{1,0:T(8,128)(4,1)S(1)}, pred[640,320]{1,0:T(8,128)(4,1)}, u32[]{:S(2)}) copy-start(pred[640,320]{1,0:T(8,128)(4,1)} %get-tuple-element.153) | copy-start | bytes 614404
  168.1 19.3 %copy-start.16 = (f32[32,512]{1,0:T(8,128)S(1)}, f32[32,512]{1,0:T(8,128)}, u32[]{:S(2)}) copy-start(f32[32,512]{1,0:T(8,128)} %copy-done.15) | copy-start | bytes 196612
  168.1 20.0 %copy-start.36 = (s32[6]{0:T(128)S(1)}, s32[6]{0:T(128)}, u32[]{:S(2)}) copy-start(s32[6]{0:T(128)} %param.15) | copy-start | bytes 76
  182.1 5.9 %collective-permute-start = (bf16[6,8,512]{2,1,0:T(8,128)(2,1)S(1)}, bf16[6,8,512]{2,1,0:T(8,128)(2,1)S(1)}, u32[]{:S(2)}, u32[]{:S(2)}) collective-permute-start(bf16[6,8,512]{2,1,0:T(8,128)(2,1)S(1)} %get-tuple-element.117), channel_id=1, source_target_pairs={{0,8},{8,16},{16,24},{1,9},{9,17},{17,25},{2,10},{10,18},{18,26},{... | collective-permute-start | bytes 147464 | tf_op jit(solution)/shard_map/ppermute | solution.py:1017
  185.2 6.0 %collective-permute-start.1 = (bf16[6,8,512]{2,1,0:T(8,128)(2,1)S(1)}, bf16[6,8,512]{2,1,0:T(8,128)(2,1)S(1)}, u32[]{:S(2)}, u32[]{:S(2)}) collective-permute-start(bf16[6,8,512]{2,1,0:T(8,128)(2,1)S(1)} %get-tuple-element.116), channel_id=1, source_target_pairs={{8,0},{16,8},{24,16},{9,1},{17,9},{25,17},{10,2},{18,10},{26,18},{... | collective-permute-start | bytes 147464 | tf_op jit(solution)/shard_map/ppermute | solution.py:1018
  191.8 60.0 %copy-start.17 = (f32[32,512]{1,0:T(8,128)S(1)}, f32[32,512]{1,0:T(8,128)}, u32[]{:S(2)}) copy-start(f32[32,512]{1,0:T(8,128)} %copy.83) | copy-start | bytes 196612
  246.2 6.4 %collective-permute-start.2 = (bf16[6,8,512]{2,1,0:T(8,128)(2,1)S(1)}, bf16[6,8,512]{2,1,0:T(8,128)(2,1)S(1)}, u32[]{:S(2)}, u32[]{:S(2)}) collective-permute-start(bf16[6,8,512]{2,1,0:T(8,128)(2,1)S(1)} %get-tuple-element.115), channel_id=1, source_target_pairs={{0,8},{8,16},{16,24},{1,9},{9,17},{17,25},{2,10},{10,18},{18,26},{... | collective-permute-start | bytes 147464 | tf_op jit(solution)/shard_map/ppermute | solution.py:1017
  250.5 6.0 %collective-permute-start.3 = (bf16[6,8,512]{2,1,0:T(8,128)(2,1)S(1)}, bf16[6,8,512]{2,1,0:T(8,128)(2,1)S(1)}, u32[]{:S(2)}, u32[]{:S(2)}) collective-permute-start(bf16[6,8,512]{2,1,0:T(8,128)(2,1)S(1)} %get-tuple-element.114), channel_id=1, source_target_pairs={{8,0},{16,8},{24,16},{9,1},{17,9},{25,17},{10,2},{18,10},{26,18},{... | collective-permute-start | bytes 147464 | tf_op jit(solution)/shard_map/ppermute | solution.py:1018
  291.3 32.4 %copy-start.23 = (f32[32,512]{1,0:T(8,128)S(1)}, f32[32,512]{1,0:T(8,128)}, u32[]{:S(2)}) copy-start(f32[32,512]{1,0:T(8,128)} %copy-done.22) | copy-start | bytes 196612
  291.3 33.5 %copy-start.7 = (f32[6,32,512]{2,1,0:T(8,128)S(1)}, f32[6,32,512]{2,1,0:T(8,128)}, u32[]{:S(2)}) copy-start(f32[6,32,512]{2,1,0:T(8,128)} %get-tuple-element.74) | copy-start | bytes 1179652
  291.3 44.7 %copy-start.3 = (f32[32,512]{1,0:T(8,128)S(1)}, f32[32,512]{1,0:T(8,128)}, u32[]{:S(2)}) copy-start(f32[32,512]{1,0:T(8,128)} %copy-done.2) | copy-start | bytes 196612
  322.9 15.3 %copy-start.18 = (f32[32,512]{1,0:T(8,128)S(1)}, f32[32,512]{1,0:T(8,128)}, u32[]{:S(2)}) copy-start(f32[32,512]{1,0:T(8,128)} %copy.82) | copy-start | bytes 196612
  322.9 15.3 %copy-start.26 = (f32[32,512]{1,0:T(8,128)S(1)}, f32[32,512]{1,0:T(8,128)}, u32[]{:S(2)}) copy-start(f32[32,512]{1,0:T(8,128)} %get-tuple-element.91) | copy-start | bytes 196612
  322.9 15.3 %copy-start.27 = (f32[32,512]{1,0:T(8,128)S(1)}, f32[32,512]{1,0:T(8,128)}, u32[]{:S(2)}) copy-start(f32[32,512]{1,0:T(8,128)} %get-tuple-element.93) | copy-start | bytes 196612
  338.3 43.7 %copy-start.32 = (f32[16,512]{1,0:T(8,128)S(1)}, f32[16,512]{1,0:T(8,128)}, u32[]{:S(2)}) copy-start(f32[16,512]{1,0:T(8,128)} %get-tuple-element.90) | copy-start | bytes 98308
  338.3 43.7 %copy-start.33 = (f32[8,512]{1,0:T(8,128)S(1)}, f32[8,512]{1,0:T(8,128)}, u32[]{:S(2)}) copy-start(f32[8,512]{1,0:T(8,128)} %get-tuple-element.88) | copy-start | bytes 49156
  382.9 4.0 copy-start.6
  383.7 4.7 copy-start.5
  388.4 3.9 copy-start.10
  389.9 4.5 copy-start.19
  395.2 117.9 %copy-start.24 = (f32[2,128,32]{1,2,0:T(8,128)S(1)}, f32[2,128,32]{1,2,0:T(8,128)}, u32[]{:S(2)}) copy-start(f32[2,128,32]{1,2,0:T(8,128)} %param.23) | copy-start | bytes 98308
  395.2 118.6 %copy-start.34 = (f32[2,32]{1,0:T(2,128)S(1)}, f32[2,32]{1,0:T(2,128)}, u32[]{:S(2)}) copy-start(f32[2,32]{1,0:T(2,128)} %param.22) | copy-start | bytes 772
  395.2 119.2 %copy-start.21 = (f32[4,32,128]{2,1,0:T(8,128)S(1)}, f32[4,32,128]{2,1,0:T(8,128)}, u32[]{:S(2)}) copy-start(f32[4,32,128]{2,1,0:T(8,128)} %multiply_exponential_fusion.1) | copy-start | bytes 196612
  510.8 14.7 %copy-start.25 = (f32[64,128]{1,0:T(8,128)}, f32[64,128]{1,0:T(8,128)S(1)}, u32[]{:S(2)}) copy-start(f32[64,128]{1,0:T(8,128)S(1)} %slice.58) | copy-start | bytes 98308
  513.8 11.7 %copy-start.35 = (f32[2,32]{1,0:T(2,128)}, f32[2,32]{1,0:T(2,128)S(1)}, u32[]{:S(2)}) copy-start(f32[2,32]{1,0:T(2,128)S(1)} %reshape_squeeze.3) | copy-start | bytes 772
  515.2 10.3 %copy-start.1 = (f32[6,128,32]{1,2,0:T(8,128)S(1)}, f32[6,128,32]{1,2,0:T(8,128)}, u32[]{:S(2)}) copy-start(f32[6,128,32]{1,2,0:T(8,128)} %param.14) | copy-start | bytes 294916
  (9 other events, 19.6 us)
